TPU v7x, 32 devices: a whole 2x2x4 slice. The times are simulated.
32 devices in a mesh: dp: 8 (over y, x, core), mp: 4 (over z).
Axes of the slice: x: 2, y: 2, z: 4, core: 2. Of those that a mesh axis runs over, the one named last changes fastest.
Arguments:
- latents: bfloat16 [32, 256, 16], P('dp'), may hold values from -6 to 6
- noise: bfloat16 [32, 256, 16], P('dp'), may hold values from -6 to 6
- labels: int32 [32], P('dp'), may hold values from 0 to 999
- time_index: int32 [32], P('dp'), may hold values from 0 to 999
- tables: float32 [1288, 768], P(None, 'dp'), may hold values from -2 to 2
- time_proj: float32 [768, 768], P('dp'), may hold values from -0.21875 to 0.21875
- modulation: float32 [768, 10752], P('dp', 'mp'), may hold values from -0.6 to 0.6
- qkv_proj: float32 [2, 768, 3, 768], P(None, 'dp', None, 'mp'), may hold values from -0.21875 to 0.21875
- out_proj: float32 [2, 768, 768], P(None, 'mp', 'dp'), may hold values from -0.875 to 0.875
- up_proj: float32 [2, 768, 3072], P(None, 'dp', 'mp'), may hold values from -0.21875 to 0.21875
- down_proj: float32 [2, 3072, 768], P(None, 'mp', 'dp'), may hold values from -0.109375 to 0.109375
- qkv_momentum: float32 [2, 768, 3, 768], P(None, 'dp', None, 'mp'), may hold values from -8.166273e-07 to 8.166273e-07
- out_momentum: float32 [2, 768, 768], P(None, 'mp', 'dp'), may hold values from -8.166273e-07 to 8.166273e-07
- up_momentum: float32 [2, 768, 3072], P(None, 'dp', 'mp'), may hold values from -8.166273e-07 to 8.166273e-07
- down_momentum: float32 [2, 3072, 768], P(None, 'mp', 'dp'), may hold values from -8.166273e-07 to 8.166273e-07
- tables_first: float32 [1288, 768], P(None, 'dp'), may hold values from -8.166273e-07 to 8.166273e-07
- tables_second: float32 [1288, 768], P(None, 'dp'), may hold values from 2.1923682e-15 to 8.7528006e-15
- time_first: float32 [768, 768], P('dp'), may hold values from -8.166273e-07 to 8.166273e-07
- time_second: float32 [768, 768], P('dp'), may hold values from 2.1923682e-15 to 8.7528006e-15
- mod_first: float32 [768, 10752], P('dp', 'mp'), may hold values from -8.166273e-07 to 8.166273e-07
- mod_second: float32 [768, 10752], P('dp', 'mp'), may hold values from 2.1923682e-15 to 8.7528006e-15
- adam_step: int32 [1], replicated, may hold values from 2 to 20
Outputs:
- loss: float32 [], replicated
- grad_norm: float32 [], replicated
- qkv_updated: float32 [2, 768, 3, 768], P(None, 'dp', None, 'mp')
- qkv_momentum_new: float32 [2, 768, 3, 768], P(None, 'dp', None, 'mp')
- out_updated: float32 [2, 768, 768], P(None, 'mp', 'dp')
- out_momentum_new: float32 [2, 768, 768], P(None, 'mp', 'dp')
- up_updated: float32 [2, 768, 3072], P(None, 'dp', 'mp')
- up_momentum_new: float32 [2, 768, 3072], P(None, 'dp', 'mp')
- down_updated: float32 [2, 3072, 768], P(None, 'mp', 'dp')
- down_momentum_new: float32 [2, 3072, 768], P(None, 'mp', 'dp')
- tables_updated: float32 [1288, 768], P(None, 'dp')
- tables_first_new: float32 [1288, 768], P(None, 'dp')
- tables_second_new: float32 [1288, 768], P(None, 'dp')
- time_updated: float32 [768, 768], P('dp')
- time_first_new: float32 [768, 768], P('dp')
- time_second_new: float32 [768, 768], P('dp')
- mod_updated: float32 [768, 10752], P('dp', 'mp')
- mod_first_new: float32 [768, 10752], P('dp', 'mp')
- mod_second_new: float32 [768, 10752], P('dp', 'mp')
All inputs are finite; a program needn't handle non-finite values.
Results may differ from a plain program's by a relative error of at most 0.014.
The roundings to bfloat16 on the way count: a program that leaves them out, or rounds other values in their place, can miss the bound.
Values may be sent and summed in bfloat16 or wider, within the bound.
No kernel may reach another device: no remote copies, remote signals or barrier semaphores. Data moves between devices by JAX's collectives and lax.ppermute only.
A program may use at most 192 MiB of HBM per device.

v0:
```python
import math

import jax
import jax.numpy as jnp
from jax import lax
from jax.sharding import PartitionSpec as P

D = 768
FF = 3072
PATCH_IN = 16
FREQ = 256
CLASSES = 1000
GRID = 16
LAYERS = 2
MICRO = 2
NS_ITERS = 5
TSTEPS = 1000
HD = 64
TOK = 256


highest = lax.Precision.HIGHEST
beta_one = 0.5
beta_two = 0.95
adam_eps = 1e-08
adam_decay = 0.01
rate_tables = 0.05
rate_time = 0.01
rate_modulation = 0.02
muon_mu = 0.5
muon_rate = 1.0
muon_decay = 0.01
clip_norm = 0.001
ns_a = 3.4445
ns_b = -4.775
ns_c = 2.0315


def freq_table(time_index):
    half_width = FREQ // 2
    rates = jnp.exp(-math.log(10000.0) * jnp.arange(half_width, dtype=jnp.float32) / half_width)
    time_value = (time_index.astype(jnp.float32) + 0.5) * (1000.0 / TSTEPS)
    angles = time_value[:, None] * rates[None, :]
    return jnp.concatenate([jnp.cos(angles), jnp.sin(angles)], axis=1)


def position_table():
    quarter = D // 4
    omega_rates = 1.0 / 10000.0 ** (jnp.arange(quarter, dtype=jnp.float32) / quarter)
    positions = jnp.arange(TOK)
    col_angle = (positions % GRID).astype(jnp.float32)[:, None] * omega_rates[None, :]
    row_angle = (positions // GRID).astype(jnp.float32)[:, None] * omega_rates[None, :]
    return jnp.concatenate(
        [jnp.sin(col_angle), jnp.cos(col_angle), jnp.sin(row_angle), jnp.cos(row_angle)], axis=1
    )


def layer_norm(stream):
    centered = stream - jnp.mean(stream, axis=-1, keepdims=True)
    inv_scale = lax.rsqrt(jnp.mean(centered * centered, axis=-1, keepdims=True) + 1e-06)
    return (centered * inv_scale, inv_scale)


def norm_back(normed, inv_scale, gradient):
    return inv_scale * (
        gradient
        - jnp.mean(gradient, axis=-1, keepdims=True)
        - normed * jnp.mean(gradient * normed, axis=-1, keepdims=True)
    )


def branch_total(partial_sum):
    return lax.psum(partial_sum, "mp")


def input_total(partial_sum):
    return lax.psum(partial_sum, "mp")


def split_heads(qkv):
    seq_count, tok_count, local_width = (qkv.shape[0], qkv.shape[1], qkv.shape[3])
    pieces = qkv.reshape(seq_count, tok_count, 3, local_width // HD, HD)
    return (pieces[:, :, 0], pieces[:, :, 1], pieces[:, :, 2])


def attend(qkv):
    queries, key_rows, values = split_heads(qkv)
    scores = jnp.einsum(
        "sqhd,skhd->shqk", queries, key_rows, preferred_element_type=jnp.float32
    ) * HD ** (-0.5)
    row_peak = jnp.max(scores, axis=-1, keepdims=True)
    exponent = jnp.exp(scores - row_peak)
    row_total = jnp.sum(exponent, axis=-1, keepdims=True)
    probs = (exponent / row_total).astype(jnp.bfloat16)
    attended = jnp.einsum(
        "shqk,skhd->sqhd", probs, values, preferred_element_type=jnp.float32
    ).astype(jnp.bfloat16)
    return (
        attended.reshape(qkv.shape[0], qkv.shape[1], qkv.shape[3]),
        row_peak + jnp.log(row_total),
    )


def attend_back(qkv, log_total, d_attended):
    queries, key_rows, values = split_heads(qkv)
    scores = jnp.einsum(
        "sqhd,skhd->shqk", queries, key_rows, preferred_element_type=jnp.float32
    ) * HD ** (-0.5)
    probs = jnp.exp(scores - log_total)
    probs_low = probs.astype(jnp.bfloat16)
    grad_heads = d_attended.reshape(queries.shape)
    d_values = jnp.einsum(
        "shqk,sqhd->skhd", probs_low, grad_heads, preferred_element_type=jnp.float32
    )
    d_probs = jnp.einsum("sqhd,skhd->shqk", grad_heads, values, preferred_element_type=jnp.float32)
    d_scores = (probs * (d_probs - jnp.sum(d_probs * probs, axis=-1, keepdims=True))).astype(
        jnp.bfloat16
    )
    d_queries = jnp.einsum(
        "shqk,skhd->sqhd", d_scores, key_rows, preferred_element_type=jnp.float32
    ) * HD ** (-0.5)
    d_keys = jnp.einsum(
        "shqk,sqhd->skhd", d_scores, queries, preferred_element_type=jnp.float32
    ) * HD ** (-0.5)
    stacked = jnp.stack([d_queries, d_keys, d_values], axis=2)
    return stacked.reshape(qkv.shape).astype(jnp.bfloat16)


def layer_forward(stream, layer_weights, layer_mods):
    w_qkv, w_out, w_up, w_down = layer_weights
    shift_a, scale_a, gate_a, shift_b, scale_b, gate_b = [
        layer_mods[:, slot, None, :] for slot in range(6)
    ]
    normed_a, inv_a = layer_norm(stream)
    in_a = (normed_a * (1.0 + scale_a) + shift_a).astype(jnp.bfloat16)
    qkv = jnp.einsum("std,dcm->stcm", in_a, w_qkv, preferred_element_type=jnp.float32).astype(
        jnp.bfloat16
    )
    attended, log_total = attend(qkv)
    branch_a = branch_total(
        jnp.einsum("stm,md->std", attended, w_out, preferred_element_type=jnp.float32)
    )
    stream_mid = stream + gate_a * branch_a
    normed_b, inv_b = layer_norm(stream_mid)
    in_b = (normed_b * (1.0 + scale_b) + shift_b).astype(jnp.bfloat16)
    hidden_pre = jnp.einsum("std,df->stf", in_b, w_up, preferred_element_type=jnp.float32)
    hidden = jax.nn.gelu(hidden_pre, approximate=True).astype(jnp.bfloat16)
    branch_b = branch_total(
        jnp.einsum("stf,fd->std", hidden, w_down, preferred_element_type=jnp.float32)
    )
    saved_layer = (
        normed_a,
        inv_a,
        in_a,
        qkv,
        log_total,
        attended,
        branch_a,
        normed_b,
        inv_b,
        in_b,
        hidden_pre,
        hidden,
        branch_b,
    )
    return (stream_mid + gate_b * branch_b, saved_layer)


def layer_backward(gradient, saved_layer, layer_weights, layer_mods):
    w_qkv, w_out, w_up, w_down = layer_weights
    (
        normed_a,
        inv_a,
        in_a,
        qkv,
        log_total,
        attended,
        branch_a,
        normed_b,
        inv_b,
        in_b,
        hidden_pre,
        hidden,
        branch_b,
    ) = saved_layer
    shift_a, scale_a, gate_a, shift_b, scale_b, gate_b = [
        layer_mods[:, slot, None, :] for slot in range(6)
    ]
    d_branch_b = (gate_b * gradient).astype(jnp.bfloat16)
    d_gate_b = jnp.sum(gradient * branch_b, axis=1)
    d_down = jnp.einsum("stf,std->fd", hidden, d_branch_b, preferred_element_type=jnp.float32)
    d_hidden = jnp.einsum("std,fd->stf", d_branch_b, w_down, preferred_element_type=jnp.float32)
    d_pre = jax.vjp(lambda value_in: jax.nn.gelu(value_in, approximate=True), hidden_pre)[1](
        d_hidden
    )[0].astype(jnp.bfloat16)
    d_up = jnp.einsum("std,stf->df", in_b, d_pre, preferred_element_type=jnp.float32)
    d_in_b = input_total(jnp.einsum("stf,df->std", d_pre, w_up, preferred_element_type=jnp.float32))
    d_scale_b = jnp.sum(d_in_b * normed_b, axis=1)
    d_shift_b = jnp.sum(d_in_b, axis=1)
    d_mid = gradient + norm_back(normed_b, inv_b, d_in_b * (1.0 + scale_b))
    d_branch_a = (gate_a * d_mid).astype(jnp.bfloat16)
    d_gate_a = jnp.sum(d_mid * branch_a, axis=1)
    d_out = jnp.einsum("stm,std->md", attended, d_branch_a, preferred_element_type=jnp.float32)
    d_attended = jnp.einsum(
        "std,md->stm", d_branch_a, w_out, preferred_element_type=jnp.float32
    ).astype(jnp.bfloat16)
    d_qkv = attend_back(qkv, log_total, d_attended)
    d_wqkv = jnp.einsum("std,stcm->dcm", in_a, d_qkv, preferred_element_type=jnp.float32)
    d_in_a = input_total(
        jnp.einsum("stcm,dcm->std", d_qkv, w_qkv, preferred_element_type=jnp.float32)
    )
    d_scale_a = jnp.sum(d_in_a * normed_a, axis=1)
    d_shift_a = jnp.sum(d_in_a, axis=1)
    grad_in = d_mid + norm_back(normed_a, inv_a, d_in_a * (1.0 + scale_a))
    d_mods = jnp.stack([d_shift_a, d_scale_a, d_gate_a, d_shift_b, d_scale_b, d_gate_b], axis=1)
    return (grad_in, d_mods, (d_wqkv, d_out, d_up, d_down))


def micro_step(latent_rows, noise_rows, label_rows, time_rows, gathered, token_count):
    table_rows, time_weight, mod_weight, qkv_all, out_all, up_all, down_all = gathered
    seq_count = latent_rows.shape[0]
    patch_w = table_rows[:PATCH_IN]
    time_in = table_rows[PATCH_IN : PATCH_IN + FREQ]
    class_table = table_rows[PATCH_IN + FREQ : PATCH_IN + FREQ + CLASSES]
    head_t = table_rows[PATCH_IN + FREQ + CLASSES :]
    freq = freq_table(time_rows).astype(jnp.bfloat16)
    time_pre = jnp.dot(freq, time_in, preferred_element_type=jnp.float32)
    time_act = jax.nn.silu(time_pre).astype(jnp.bfloat16)
    onehot = (label_rows[:, None] == jnp.arange(CLASSES)[None, :]).astype(jnp.bfloat16)
    condition = jnp.dot(time_act, time_weight, preferred_element_type=jnp.float32) + jnp.dot(
        onehot, class_table, preferred_element_type=jnp.float32
    )
    cond_act = jax.nn.silu(condition).astype(jnp.bfloat16)
    mod_rows = lax.all_gather(
        jnp.dot(cond_act, mod_weight, preferred_element_type=jnp.float32), "mp", axis=1, tiled=True
    )
    times = ((time_rows.astype(jnp.float32) + 0.5) / TSTEPS)[:, None, None]
    latents_f = latent_rows.astype(jnp.float32)
    noise_f = noise_rows.astype(jnp.float32)
    noisy = ((1.0 - times) * latents_f + times * noise_f).astype(jnp.bfloat16)
    target = noise_f - latents_f
    stream = (
        jnp.einsum("stp,pd->std", noisy, patch_w, preferred_element_type=jnp.float32)
        + position_table()[None]
    )
    saved_all = []
    for layer_index in range(LAYERS):
        layer_weights = (
            qkv_all[layer_index],
            out_all[layer_index],
            up_all[layer_index],
            down_all[layer_index],
        )
        layer_mods = mod_rows[:, layer_index * 6 * D : (layer_index + 1) * 6 * D].reshape(
            seq_count, 6, D
        )
        stream, saved_layer = layer_forward(stream, layer_weights, layer_mods)
        saved_all.append(saved_layer)
    base = 6 * LAYERS * D
    shift_f = mod_rows[:, None, base : base + D]
    scale_f = mod_rows[:, None, base + D : base + 2 * D]
    normed_f, inv_f = layer_norm(stream)
    in_f = (normed_f * (1.0 + scale_f) + shift_f).astype(jnp.bfloat16)
    output = jnp.einsum("std,pd->stp", in_f, head_t, preferred_element_type=jnp.float32)
    weight_t = 0.5 + times
    velocity_miss = output - target
    loss_part = jnp.sum(weight_t * velocity_miss * velocity_miss) / token_count
    d_output = (2.0 * weight_t * velocity_miss / token_count).astype(jnp.bfloat16)
    d_head = jnp.einsum("stp,std->pd", d_output, in_f, preferred_element_type=jnp.float32)
    d_in_f = jnp.einsum("stp,pd->std", d_output, head_t, preferred_element_type=jnp.float32)
    d_scale_f = jnp.sum(d_in_f * normed_f, axis=1)
    d_shift_f = jnp.sum(d_in_f, axis=1)
    gradient = norm_back(normed_f, inv_f, d_in_f * (1.0 + scale_f))
    layer_grads = [None] * LAYERS
    mod_grads = [None] * LAYERS
    for layer_index in reversed(range(LAYERS)):
        layer_weights = (
            qkv_all[layer_index],
            out_all[layer_index],
            up_all[layer_index],
            down_all[layer_index],
        )
        layer_mods = mod_rows[:, layer_index * 6 * D : (layer_index + 1) * 6 * D].reshape(
            seq_count, 6, D
        )
        gradient, d_mods, d_weights = layer_backward(
            gradient, saved_all[layer_index], layer_weights, layer_mods
        )
        layer_grads[layer_index] = d_weights
        mod_grads[layer_index] = d_mods.reshape(seq_count, 6 * D)
    d_first = gradient.astype(jnp.bfloat16)
    d_patch = jnp.einsum("stp,std->pd", noisy, d_first, preferred_element_type=jnp.float32)
    d_mod_all = jnp.concatenate(mod_grads + [d_shift_f, d_scale_f], axis=1).astype(jnp.bfloat16)
    mod_width = mod_weight.shape[1]
    d_mod_own = lax.dynamic_slice_in_dim(d_mod_all, lax.axis_index("mp") * mod_width, mod_width, 1)
    d_modulation = jnp.einsum("sd,sm->dm", cond_act, d_mod_own, preferred_element_type=jnp.float32)
    d_cond_act = lax.psum(
        jnp.einsum("sm,dm->sd", d_mod_own, mod_weight, preferred_element_type=jnp.float32), "mp"
    )
    d_condition = jax.vjp(jax.nn.silu, condition)[1](d_cond_act)[0].astype(jnp.bfloat16)
    d_class = jnp.einsum("sc,sd->cd", onehot, d_condition, preferred_element_type=jnp.float32)
    d_time_weight = jnp.einsum(
        "se,sd->ed", time_act, d_condition, preferred_element_type=jnp.float32
    )
    d_time_act = jnp.einsum(
        "sd,ed->se", d_condition, time_weight, preferred_element_type=jnp.float32
    )
    d_time_pre = jax.vjp(jax.nn.silu, time_pre)[1](d_time_act)[0].astype(jnp.bfloat16)
    d_time_in = jnp.einsum("sf,sd->fd", freq, d_time_pre, preferred_element_type=jnp.float32)
    d_tables = jnp.concatenate([d_patch, d_time_in, d_class, d_head], axis=0)
    stacked = tuple(
        (
            jnp.stack([layer_grads[layer_index][slot] for layer_index in range(LAYERS)])
            for slot in range(4)
        )
    )
    return (loss_part, (d_tables, d_time_weight, d_modulation) + stacked)


def gram_product(matrix):
    return lax.psum(jnp.dot(matrix, matrix.T, precision=highest), "mp")


def orthogonalize(matrix):
    square = gram_product(matrix)
    frobenius = jnp.sqrt(jnp.trace(square)) + 1e-07
    matrix = matrix / frobenius
    square = square / (frobenius * frobenius)
    for iteration in range(NS_ITERS):
        if iteration > 0:
            square = gram_product(matrix)
        poly_term = ns_b * square + ns_c * jnp.dot(square, square, precision=highest)
        matrix = ns_a * matrix + jnp.dot(poly_term, matrix, precision=highest)
    return matrix


def adam_update(weight, gradient, first, second, rate, step_value):
    first_new = beta_one * first + (1.0 - beta_one) * gradient
    second_new = beta_two * second + (1.0 - beta_two) * gradient * gradient
    first_hat = first_new / (1.0 - jnp.power(beta_one, step_value))
    second_hat = second_new / (1.0 - jnp.power(beta_two, step_value))
    updated = weight * (1.0 - rate * adam_decay) - rate * first_hat / (
        jnp.sqrt(second_hat) + adam_eps
    )
    return (updated, first_new, second_new)


def body(
    latents,
    noise,
    labels,
    time_index,
    tables,
    time_proj,
    modulation,
    qkv_proj,
    out_proj,
    up_proj,
    down_proj,
    qkv_momentum,
    out_momentum,
    up_momentum,
    down_momentum,
    tables_first,
    tables_second,
    time_first,
    time_second,
    mod_first,
    mod_second,
    adam_step,
):
    low_weights = tuple(
        (
            weight.astype(jnp.bfloat16)
            for weight in (tables, time_proj, modulation, qkv_proj, out_proj, up_proj, down_proj)
        )
    )
    gathered = (
        lax.all_gather(low_weights[0], "dp", axis=1, tiled=True),
        lax.all_gather(low_weights[1], "dp", axis=0, tiled=True),
        lax.all_gather(low_weights[2], "dp", axis=0, tiled=True),
        lax.all_gather(low_weights[3], "dp", axis=1, tiled=True),
        lax.all_gather(low_weights[4], "dp", axis=2, tiled=True),
        lax.all_gather(low_weights[5], "dp", axis=1, tiled=True),
        lax.all_gather(low_weights[6], "dp", axis=2, tiled=True),
    )
    per_micro = latents.shape[0] // MICRO
    token_count = per_micro * MICRO * lax.axis_size("dp") * TOK * PATCH_IN
    loss_sum = jnp.zeros((), jnp.float32)
    grad_sums = None
    for micro_index in range(MICRO):
        first_row = micro_index * per_micro
        loss_part, grad_parts = micro_step(
            latents[first_row : first_row + per_micro],
            noise[first_row : first_row + per_micro],
            labels[first_row : first_row + per_micro],
            time_index[first_row : first_row + per_micro],
            gathered,
            token_count,
        )
        loss_sum = loss_sum + loss_part
        grad_sums = (
            grad_parts if grad_sums is None else jax.tree.map(jnp.add, grad_sums, grad_parts)
        )
    reduced = (
        lax.psum_scatter(grad_sums[0], "dp", scatter_dimension=1, tiled=True),
        lax.psum_scatter(grad_sums[1], "dp", scatter_dimension=0, tiled=True),
        lax.psum_scatter(grad_sums[2], "dp", scatter_dimension=0, tiled=True),
        lax.psum_scatter(grad_sums[3], "dp", scatter_dimension=1, tiled=True),
        lax.psum_scatter(grad_sums[4], "dp", scatter_dimension=2, tiled=True),
        lax.psum_scatter(grad_sums[5], "dp", scatter_dimension=1, tiled=True),
        lax.psum_scatter(grad_sums[6], "dp", scatter_dimension=2, tiled=True),
    )
    grad_tables, grad_time, grad_mod, grad_qkv, grad_out, grad_up, grad_down = reduced
    mp_count = lax.axis_size("mp")
    shared_square = (jnp.sum(grad_tables * grad_tables) + jnp.sum(grad_time * grad_time)) / mp_count
    own_square = sum(
        (
            jnp.sum(gradient * gradient)
            for gradient in (grad_mod, grad_qkv, grad_out, grad_up, grad_down)
        )
    )
    square_total, loss = lax.psum((shared_square + own_square, loss_sum / mp_count), ("dp", "mp"))
    grad_norm = jnp.sqrt(square_total)
    factor = jnp.minimum(1.0, clip_norm / (grad_norm + 1e-06))
    grad_tables, grad_time, grad_mod, grad_qkv, grad_out, grad_up, grad_down = [
        gradient * factor for gradient in reduced
    ]
    step_value = adam_step[0].astype(jnp.float32)
    tables_updated, tables_first_new, tables_second_new = adam_update(
        tables, grad_tables, tables_first, tables_second, rate_tables, step_value
    )
    time_updated, time_first_new, time_second_new = adam_update(
        time_proj, grad_time, time_first, time_second, rate_time, step_value
    )
    mod_updated, mod_first_new, mod_second_new = adam_update(
        modulation, grad_mod, mod_first, mod_second, rate_modulation, step_value
    )
    momenta_new = [
        muon_mu * momentum + gradient
        for momentum, gradient in (
            (qkv_momentum, grad_qkv),
            (out_momentum, grad_out),
            (up_momentum, grad_up),
            (down_momentum, grad_down),
        )
    ]
    nesterov = [
        gradient + muon_mu * momentum
        for gradient, momentum in zip((grad_qkv, grad_out, grad_up, grad_down), momenta_new)
    ]
    row_count = qkv_proj.shape[1]
    width_qkv = 3 * qkv_proj.shape[3]
    width_out = out_proj.shape[1]
    width_up = up_proj.shape[2]
    width_down = down_proj.shape[1]
    padded_cols = max(width_qkv, width_out, width_up, width_down)
    matrix_count = 4 * LAYERS

    def pad_cols(matrix):
        return jnp.pad(matrix, ((0, 0), (0, padded_cols - matrix.shape[1])))

    oriented = []
    for layer_index in range(LAYERS):
        oriented.append(pad_cols(nesterov[0][layer_index].reshape(row_count, width_qkv)))
        oriented.append(pad_cols(nesterov[1][layer_index].T))
        oriented.append(pad_cols(nesterov[2][layer_index]))
        oriented.append(pad_cols(nesterov[3][layer_index].T))
    stacked = jnp.stack(oriented)
    dp_count = lax.axis_size("dp")
    copies = dp_count // matrix_count
    piece_cols = padded_cols // copies
    everything = lax.all_gather(stacked, "dp", axis=1, tiled=True)
    own_matrix = lax.dynamic_index_in_dim(
        everything, lax.axis_index("dp") % matrix_count, 0, keepdims=False
    )
    ortho_own = orthogonalize(own_matrix)
    blocked = ortho_own.reshape(dp_count, row_count, copies, piece_cols)
    own_piece = lax.dynamic_index_in_dim(
        blocked, lax.axis_index("dp") // matrix_count, 2, keepdims=False
    )
    received = lax.all_to_all(
        own_piece.reshape(dp_count * row_count, piece_cols),
        "dp",
        split_axis=0,
        concat_axis=0,
        tiled=True,
    )
    returned = (
        received.reshape(copies, matrix_count, row_count, piece_cols)
        .transpose(1, 2, 0, 3)
        .reshape(matrix_count, row_count, padded_cols)
    )
    ortho_qkv = jnp.stack(
        [
            returned[4 * layer_index][:, :width_qkv].reshape(row_count, 3, width_qkv // 3)
            for layer_index in range(LAYERS)
        ]
    )
    ortho_out = jnp.stack(
        [returned[4 * layer_index + 1][:, :width_out].T for layer_index in range(LAYERS)]
    )
    ortho_up = jnp.stack([returned[4 * layer_index + 2] for layer_index in range(LAYERS)])
    ortho_down = jnp.stack([returned[4 * layer_index + 3].T for layer_index in range(LAYERS)])
    keep_factor = 1.0 - muon_rate * muon_decay
    qkv_updated = qkv_proj * keep_factor - muon_rate * ortho_qkv
    out_updated = out_proj * keep_factor - muon_rate * ortho_out
    up_updated = up_proj * keep_factor - muon_rate * ortho_up
    down_updated = down_proj * keep_factor - muon_rate * math.sqrt(max(1.0, FF / D)) * ortho_down
    return (
        loss,
        grad_norm,
        qkv_updated,
        momenta_new[0],
        out_updated,
        momenta_new[1],
        up_updated,
        momenta_new[2],
        down_updated,
        momenta_new[3],
        tables_updated,
        tables_first_new,
        tables_second_new,
        time_updated,
        time_first_new,
        time_second_new,
        mod_updated,
        mod_first_new,
        mod_second_new,
    )


def solution(mesh):
    return jax.shard_map(
        body,
        mesh=mesh,
        in_specs=(
            P("dp", None, None),
            P("dp", None, None),
            P("dp"),
            P("dp"),
            P(None, "dp"),
            P("dp", None),
            P("dp", "mp"),
            P(None, "dp", None, "mp"),
            P(None, "mp", "dp"),
            P(None, "dp", "mp"),
            P(None, "mp", "dp"),
            P(None, "dp", None, "mp"),
            P(None, "mp", "dp"),
            P(None, "dp", "mp"),
            P(None, "mp", "dp"),
            P(None, "dp"),
            P(None, "dp"),
            P("dp", None),
            P("dp", None),
            P("dp", "mp"),
            P("dp", "mp"),
            P(),
        ),
        out_specs=(
            P(),
            P(),
            P(None, "dp", None, "mp"),
            P(None, "dp", None, "mp"),
            P(None, "mp", "dp"),
            P(None, "mp", "dp"),
            P(None, "dp", "mp"),
            P(None, "dp", "mp"),
            P(None, "mp", "dp"),
            P(None, "mp", "dp"),
            P(None, "dp"),
            P(None, "dp"),
            P(None, "dp"),
            P("dp", None),
            P("dp", None),
            P("dp", None),
            P("dp", "mp"),
            P("dp", "mp"),
            P("dp", "mp"),
        ),
        check_vma=False,
    )
```

profile of v0, /device:TPU:0, one launch (start us, length us, event | category | flops | bytes accessed | tf_op | source)
XLA Modules:
  0.0 2524.1 jit_solution(2619447781012430874)
XLA Ops:
  81.3 19.9 all-gather.10.cloned.1.call-done
  107.9 32.0 %all-gather.12.cloned.1.call-done = bf16[768,2688]{1,0:T(8,128)(2,1)} async-done(((bf16[96,2688]{1,0:T(8,128)(2,1)}), bf16[768,2688]{1,0:T(8,128)(2,1)}) %all-gather.12.cloned.1.call-update) | async-done | bytes 4128784 | tf_op jit(solution)/shard_map/all_gather | solution.py:381
  212.0 99.5 %all-reduce.58.cloned.1.call-done = (f32[2,256,768]{2,1,0:T(8,128)}, f32[2,256,768]{2,1,0:T(8,128)}) async-done(((f32[2,256,768]{2,1,0:T(8,128)}, f32[2,256,768]{2,1,0:T(8,128)}), (f32[2,256,768]{2,1,0:T(8,128)}, f32[2,256,768]{2,1,0:T(8,128)})) %all-reduce.58.cloned.1.call-update) | async-done | bytes 3145744 | tf_op jit(solution)/shard_map/psum | solution.py:73
  317.5 24.4 all-gather.16.cloned.1.call-done
  370.7 101.8 %all-reduce.56.cloned.1.call-done = (f32[2,256,768]{2,1,0:T(8,128)}, f32[2,256,768]{2,1,0:T(8,128)}) async-done(((f32[2,256,768]{2,1,0:T(8,128)}, f32[2,256,768]{2,1,0:T(8,128)}), (f32[2,256,768]{2,1,0:T(8,128)}, f32[2,256,768]{2,1,0:T(8,128)})) %all-reduce.56.cloned.1.call-update) | async-done | bytes 3145744 | tf_op jit(solution)/shard_map/psum | solution.py:73
  496.3 110.5 %all-reduce.54.cloned.1.call-done = (f32[2,256,768]{2,1,0:T(8,128)}, f32[2,256,768]{2,1,0:T(8,128)}) async-done(((f32[2,256,768]{2,1,0:T(8,128)}, f32[2,256,768]{2,1,0:T(8,128)}), (f32[2,256,768]{2,1,0:T(8,128)}, f32[2,256,768]{2,1,0:T(8,128)})) %all-reduce.54.cloned.1.call-update) | async-done | bytes 3145744 | tf_op jit(solution)/shard_map/psum | solution.py:73
  624.0 117.1 %all-reduce.52.cloned.1.call-done = (f32[2,256,768]{2,1,0:T(8,128)}, f32[2,256,768]{2,1,0:T(8,128)}) async-done(((f32[2,256,768]{2,1,0:T(8,128)}, f32[2,256,768]{2,1,0:T(8,128)}), (f32[2,256,768]{2,1,0:T(8,128)}, f32[2,256,768]{2,1,0:T(8,128)})) %all-reduce.52.cloned.1.call-update) | async-done | bytes 3145744 | tf_op jit(solution)/shard_map/psum | solution.py:73
  766.9 119.6 %all-reduce.50.cloned.1.call-done = (f32[2,256,768]{2,1,0:T(8,128)}, f32[2,256,768]{2,1,0:T(8,128)}) async-done(((f32[2,256,768]{2,1,0:T(8,128)}, f32[2,256,768]{2,1,0:T(8,128)}), (f32[2,256,768]{2,1,0:T(8,128)}, f32[2,256,768]{2,1,0:T(8,128)})) %all-reduce.50.cloned.1.call-update) | async-done | bytes 3145744 | tf_op jit(solution)/shard_map/psum | solution.py:77
  908.3 120.0 %all-reduce.48.cloned.1.call-done = (f32[2,256,768]{2,1,0:T(8,128)}, f32[2,256,768]{2,1,0:T(8,128)}) async-done(((f32[2,256,768]{2,1,0:T(8,128)}, f32[2,256,768]{2,1,0:T(8,128)}), (f32[2,256,768]{2,1,0:T(8,128)}, f32[2,256,768]{2,1,0:T(8,128)})) %all-reduce.48.cloned.1.call-update) | async-done | bytes 3145744 | tf_op jit(solution)/shard_map/psum | solution.py:77
  1047.4 119.5 %all-reduce.46.cloned.1.call-done = (f32[2,256,768]{2,1,0:T(8,128)}, f32[2,256,768]{2,1,0:T(8,128)}) async-done(((f32[2,256,768]{2,1,0:T(8,128)}, f32[2,256,768]{2,1,0:T(8,128)}), (f32[2,256,768]{2,1,0:T(8,128)}, f32[2,256,768]{2,1,0:T(8,128)})) %all-reduce.46.cloned.1.call-update) | async-done | bytes 3145744 | tf_op jit(solution)/shard_map/psum | solution.py:77
  1269.4 40.8 %all-reduce.44.cloned.1.call-done = (f32[2,256,768]{2,1,0:T(8,128)}, f32[2,256,768]{2,1,0:T(8,128)}) async-done(((f32[2,256,768]{2,1,0:T(8,128)}, f32[2,256,768]{2,1,0:T(8,128)}), (f32[2,256,768]{2,1,0:T(8,128)}, f32[2,256,768]{2,1,0:T(8,128)})) %all-reduce.44.cloned.1.call-update) | async-done | bytes 3145744 | tf_op jit(solution)/shard_map/psum | solution.py:77
  1367.6 82.9 %all-reduce.42.cloned.1.call-done = (f32[2,768,768]{2,0,1:T(2,128)}, f32[2,768,768]{1,0,2:T(2,128)}) async-done(((f32[2,768,768]{2,0,1:T(2,128)}, f32[2,768,768]{1,0,2:T(2,128)}), (f32[2,768,768]{2,0,1:T(2,128)}, f32[2,768,768]{1,0,2:T(2,128)})) %all-reduce.42.cloned.1.call-update) | async-done | bytes 9437200
  1456.9 33.4 %reduce-scatter.20.cloned.1.call-done = f32[96,384]{1,0:T(8,128)} async-done(((f32[768,384]{1,0:T(8,128)}), f32[96,384]{1,0:T(8,128)}) %reduce-scatter.20.cloned.1.call-update) | async-done | bytes 147472
  1492.2 49.4 %reduce-scatter.18.cloned.1.call-done = f32[96,1152]{1,0:T(8,128)} async-done(((f32[768,1152]{1,0:T(8,128)}), f32[96,1152]{1,0:T(8,128)}) %reduce-scatter.18.cloned.1.call-update) | async-done | bytes 442384
  1544.3 43.0 %reduce-scatter.12.cloned.1.call-done = f32[96,768]{1,0:T(8,128)} async-done(((f32[768,768]{1,0:T(8,128)}), f32[96,768]{1,0:T(8,128)}) %reduce-scatter.12.cloned.1.call-update) | async-done | bytes 294928 | tf_op jit(solution)/shard_map/reduce_scatter | solution.py:407
  1588.9 53.7 %reduce-scatter.16.cloned.1.call-done = f32[96,1288]{1,0:T(8,128)} async-done(((f32[768,1288]{1,0:T(8,128)}), f32[96,1288]{1,0:T(8,128)}) %reduce-scatter.16.cloned.1.call-update) | async-done | bytes 494608
  1646.0 71.0 %reduce-scatter.14.cloned.1.call-done = f32[96,2688]{1,0:T(8,128)} async-done(((f32[768,2688]{1,0:T(8,128)}), f32[96,2688]{1,0:T(8,128)}) %reduce-scatter.14.cloned.1.call-update) | async-done | bytes 1032208 | tf_op jit(solution)/shard_map/reduce_scatter | solution.py:408
  1723.7 39.3 %all-reduce.6 = (f32[]{:T(128)}, f32[]{:T(128)}) all-reduce(f32[]{:T(128)S(6)} %div.326, f32[]{:T(128)S(6)} %add.745), channel_id=1, replica_groups=mesh['dp'=8,'mp'=4] {'dp','mp'}, use_global_device_ids=true, to_apply=%region_38.39 | all-reduce | flops 2 | bytes 16 | tf_op jit(solution)/shard_map/psum | solution.py:423
  1778.4 99.6 %all-gather.20.cloned.1.call-done = f32[8,768,768]{2,0,1:T(8,128)} async-done(((f32[8,96,768]{2,0,1:T(8,128)}), f32[8,768,768]{2,0,1:T(8,128)}) %all-gather.20.cloned.1.call-update) | async-done | bytes 18874384 | tf_op jit(solution)/shard_map/all_gather | solution.py:473
  1893.6 94.5 %all-reduce.32.cloned.1.call-done = f32[768,768]{1,0:T(8,128)} async-done(((f32[768,768]{1,0:T(8,128)}), f32[768,768]{1,0:T(8,128)}) %all-reduce.32.cloned.1.call-update) | async-done | bytes 2359312 | tf_op jit(solution)/shard_map/psum | solution.py:321
  2013.0 93.8 %all-reduce.34.cloned.1.call-done = f32[768,768]{1,0:T(8,128)} async-done(((f32[768,768]{1,0:T(8,128)}), f32[768,768]{1,0:T(8,128)}) %all-reduce.34.cloned.1.call-update) | async-done | bytes 2359312 | tf_op jit(solution)/shard_map/psum | solution.py:321
  2128.8 93.8 %all-reduce.36.cloned.1.call-done = f32[768,768]{1,0:T(8,128)} async-done(((f32[768,768]{1,0:T(8,128)}), f32[768,768]{1,0:T(8,128)}) %all-reduce.36.cloned.1.call-update) | async-done | bytes 2359312 | tf_op jit(solution)/shard_map/psum | solution.py:321
  2246.6 93.8 %all-reduce.38.cloned.1.call-done = f32[768,768]{1,0:T(8,128)} async-done(((f32[768,768]{1,0:T(8,128)}), f32[768,768]{1,0:T(8,128)}) %all-reduce.38.cloned.1.call-update) | async-done | bytes 2359312 | tf_op jit(solution)/shard_map/psum | solution.py:321
  2362.4 93.8 %all-reduce.40.cloned.1.call-done = f32[768,768]{1,0:T(8,128)} async-done(((f32[768,768]{1,0:T(8,128)}), f32[768,768]{1,0:T(8,128)}) %all-reduce.40.cloned.1.call-update) | async-done | bytes 2359312 | tf_op jit(solution)/shard_map/psum | solution.py:321
  (1174 shorter events, 649.0 us)
Async XLA Ops:
  11.5 89.7 %all-gather.10.cloned.1.call-start = ((), (), s32[]{:S(2)}) async-start(), calls=%async_computation.7 | async-start | bytes 1327104 | tf_op jit(solution)/shard_map/all_gather | solution.py:380
  12.3 127.6 %all-gather.12.cloned.1.call-start = ((), (), s32[]{:S(2)}) async-start(), calls=%async_computation.8 | async-start | bytes 4644864 | tf_op jit(solution)/shard_map/all_gather | solution.py:381
  13.2 179.2 %all-gather.18.cloned.1.call-start = ((), (), s32[]{:S(2)}) async-start(), calls=%async_computation.11 | async-start | bytes 2654208 | tf_op jit(solution)/shard_map/all_gather | solution.py:385
  14.5 297.1 %all-reduce.58.cloned.1.call-start = ((), (), s32[]{:S(2)}) async-start(), calls=%async_computation.31 | async-start | bytes 6291456 | tf_op jit(solution)/shard_map/psum | solution.py:73
  190.5 151.5 %all-gather.16.cloned.1.call-start = ((), (), s32[]{:S(2)}) async-start(), calls=%async_computation.10 | async-start | bytes 2654208 | tf_op jit(solution)/shard_map/all_gather | solution.py:384
  192.4 280.2 %all-reduce.56.cloned.1.call-start = ((), (), s32[]{:S(2)}) async-start(), calls=%async_computation.30 | async-start | bytes 6291456 | tf_op jit(solution)/shard_map/psum | solution.py:73
  351.3 255.4 %all-reduce.54.cloned.1.call-start = ((), (), s32[]{:S(2)}) async-start(), calls=%async_computation.29 | async-start | bytes 6291456 | tf_op jit(solution)/shard_map/psum | solution.py:73
  486.5 254.5 %all-reduce.52.cloned.1.call-start = ((), (), s32[]{:S(2)}) async-start(), calls=%async_computation.28 | async-start | bytes 6291456 | tf_op jit(solution)/shard_map/psum | solution.py:73
  620.8 265.7 %all-reduce.50.cloned.1.call-start = ((), (), s32[]{:S(2)}) async-start(), calls=%async_computation.27 | async-start | bytes 6291456 | tf_op jit(solution)/shard_map/psum | solution.py:77
  766.2 262.0 %all-reduce.48.cloned.1.call-start = ((), (), s32[]{:S(2)}) async-start(), calls=%async_computation.26 | async-start | bytes 6291456 | tf_op jit(solution)/shard_map/psum | solution.py:77
  908.0 258.9 %all-reduce.46.cloned.1.call-start = ((), (), s32[]{:S(2)}) async-start(), calls=%async_computation.25 | async-start | bytes 6291456 | tf_op jit(solution)/shard_map/psum | solution.py:77
  1046.7 263.5 %all-reduce.44.cloned.1.call-start = ((), (), s32[]{:S(2)}) async-start(), calls=%async_computation.24 | async-start | bytes 6291456 | tf_op jit(solution)/shard_map/psum | solution.py:77
  1190.0 260.5 %all-reduce.42.cloned.1.call-start = ((), (), s32[]{:S(2)}) async-start(), calls=%async_computation.23 | async-start | bytes 18874368
  1223.4 266.9 %reduce-scatter.20.cloned.1.call-start = ((), (), s32[]{:S(2)}) async-start(), calls=%async_computation.22 | async-start | bytes 1327104
  1241.9 299.8 %reduce-scatter.18.cloned.1.call-start = ((), (), s32[]{:S(2)}) async-start(), calls=%async_computation.21 | async-start | bytes 3981312
  1268.7 318.6 %reduce-scatter.12.cloned.1.call-start = ((), (), s32[]{:S(2)}) async-start(), calls=%async_computation.12 | async-start | bytes 2654208 | tf_op jit(solution)/shard_map/reduce_scatter | solution.py:407
  1337.6 305.0 %reduce-scatter.16.cloned.1.call-start = ((), (), s32[]{:S(2)}) async-start(), calls=%async_computation.20 | async-start | bytes 4866048
  1355.7 361.4 %reduce-scatter.14.cloned.1.call-start = ((), (), s32[]{:S(2)}) async-start(), calls=%async_computation.13 | async-start | bytes 9289728 | tf_op jit(solution)/shard_map/reduce_scatter | solution.py:408
  1361.7 516.4 %all-gather.20.cloned.1.call-start = ((), (), s32[]{:S(2)}) async-start(), calls=%async_computation.14 | async-start | bytes 21233664 | tf_op jit(solution)/shard_map/all_gather | solution.py:473
  1778.4 209.8 %all-reduce.32.cloned.1.call-start = ((), (), s32[]{:S(2)}) async-start(), calls=%async_computation.15 | async-start | bytes 4718592 | tf_op jit(solution)/shard_map/psum | solution.py:321
  1893.4 213.3 %all-reduce.34.cloned.1.call-start = ((), (), s32[]{:S(2)}) async-start(), calls=%async_computation.16 | async-start | bytes 4718592 | tf_op jit(solution)/shard_map/psum | solution.py:321
  2012.9 209.7 %all-reduce.36.cloned.1.call-start = ((), (), s32[]{:S(2)}) async-start(), calls=%async_computation.17 | async-start | bytes 4718592 | tf_op jit(solution)/shard_map/psum | solution.py:321
  2128.8 211.6 %all-reduce.38.cloned.1.call-start = ((), (), s32[]{:S(2)}) async-start(), calls=%async_computation.18 | async-start | bytes 4718592 | tf_op jit(solution)/shard_map/psum | solution.py:321
  2246.5 209.7 %all-reduce.40.cloned.1.call-start = ((), (), s32[]{:S(2)}) async-start(), calls=%async_computation.19 | async-start | bytes 4718592 | tf_op jit(solution)/shard_map/psum | solution.py:321
  (379 other events, 5674.0 us)
Sparse Core Ops, SparseCore 0:
  10.5 33.7 all-gather.13
  46.7 28.0 all-gather.7
  103.5 36.2 all-gather.11
  142.2 28.8 all-gather.17
  190.6 120.8 all-reduce.57
  351.4 121.0 all-reduce.55
  486.6 120.0 all-reduce.53
  620.9 120.0 all-reduce.51
  766.4 120.0 all-reduce.49
  908.2 120.0 all-reduce.47
  1046.9 120.0 all-reduce.45
  1190.1 120.0 all-reduce.43
  1313.8 136.6 all-reduce.41
  1453.6 36.7 reduce-scatter.19
  1493.7 47.9 reduce-scatter.17
  1544.9 42.3 reduce-scatter.11
  1590.7 51.9 reduce-scatter.15
  1646.1 70.8 reduce-scatter.13
  1778.5 99.5 all-gather.19
  1893.5 94.6 all-reduce.31
  2013.0 93.6 all-reduce.33
  2128.9 93.6 all-reduce.35
  2246.6 93.6 all-reduce.37
  2362.5 93.6 all-reduce.39
  (2 shorter events, 51.7 us)
where the time goes:
time: 2530 us; the launch traced here: 2520 us
  waiting for transfers between devices  1830 us (72%)
  matrix products  233 us (9%)
  local copies, waits for them, and re-layouts  221 us (9%)
  other arithmetic  103 us (4%)
  blocking collectives  96.7 us (4%)
  between operations  28 us (1%)
    psum x5, waiting for transfers between devices, gram_product(): return lax.psum(jnp.dot(matrix, matrix.T, precision=highest), 'mp')  470 us
    psum x4, waiting for transfers between devices, branch_total(): return lax.psum(partial_sum, 'mp')  429 us
    psum x4, waiting for transfers between devices, input_total(): return lax.psum(partial_sum, 'mp')  400 us
    unnamed x30, waiting for transfers between devices  220 us
    unnamed x841, local copies, waits for them, and re-layouts  163 us
    all_gather x1, waiting for transfers between devices, body(): everything = lax.all_gather(stacked, 'dp', axis=1, tiled=True)  99.6 us
    reduce_scatter x1, waiting for transfers between devices, body(): lax.psum_scatter(grad_sums[2], 'dp', scatter_dimension=0, tiled=True)  71 us
  transfers between devices with their start and end apart: 27, of which 25 were waited for; matrix products, arithmetic and copies ran while one was open for 10% of the time, Pallas kernels for 0%

commit v1 on v0

v1 whole, which is shorter than its diff:
```python
import math

import jax
import jax.numpy as jnp
from jax import lax
from jax.experimental import pallas as pl
from jax.experimental.pallas import tpu as pltpu
from jax.sharding import Mesh
from jax.sharding import PartitionSpec as P

D = 768
FF = 3072
PATCH_IN = 16
FREQ = 256
CLASSES = 1000
GRID = 16
LAYERS = 2
NS_ITERS = 5
TSTEPS = 1000
HD = 64
TOK = 256


highest = lax.Precision.HIGHEST
DP = ("dh", "dm", "pr")
ALL = ("dh", "dm", "pr", "mp")
MATS = ("dh", "mp", "dm", "pr")
beta_one = 0.5
beta_two = 0.95
adam_eps = 1e-08
adam_decay = 0.01
rate_tables = 0.05
rate_time = 0.01
rate_modulation = 0.02
muon_mu = 0.5
muon_rate = 1.0
muon_decay = 0.01
clip_norm = 0.001
ns_a = 3.4445
ns_b = -4.775
ns_c = 2.0315


def freq_table(time_index):
    half_width = FREQ // 2
    rates = jnp.exp(-math.log(10000.0) * jnp.arange(half_width, dtype=jnp.float32) / half_width)
    time_value = (time_index.astype(jnp.float32) + 0.5) * (1000.0 / TSTEPS)
    angles = time_value[:, None] * rates[None, :]
    return jnp.concatenate([jnp.cos(angles), jnp.sin(angles)], axis=1)


def position_table():
    quarter = D // 4
    omega_rates = 1.0 / 10000.0 ** (jnp.arange(quarter, dtype=jnp.float32) / quarter)
    positions = jnp.arange(TOK)
    col_angle = (positions % GRID).astype(jnp.float32)[:, None] * omega_rates[None, :]
    row_angle = (positions // GRID).astype(jnp.float32)[:, None] * omega_rates[None, :]
    return jnp.concatenate(
        [jnp.sin(col_angle), jnp.cos(col_angle), jnp.sin(row_angle), jnp.cos(row_angle)], axis=1
    )


def layer_norm(stream):
    centered = stream - jnp.mean(stream, axis=-1, keepdims=True)
    inv_scale = lax.rsqrt(jnp.mean(centered * centered, axis=-1, keepdims=True) + 1e-06)
    return (centered * inv_scale, inv_scale)


def norm_back(normed, inv_scale, gradient):
    return inv_scale * (
        gradient
        - jnp.mean(gradient, axis=-1, keepdims=True)
        - normed * jnp.mean(gradient * normed, axis=-1, keepdims=True)
    )


def axis_bits(axis):
    return [(axis, bit) for bit in reversed(range(int(math.log2(lax.axis_size(axis)))))]


def own_bit(stage):
    axis, bit = stage
    return (lax.axis_index(axis) >> bit) & 1


def swap(value, stage):
    axis, bit = stage
    return lax.ppermute(
        value, axis, [(place, place ^ (1 << bit)) for place in range(lax.axis_size(axis))]
    )


def exchange_sum(value, stages):
    for stage in stages:
        value = value + swap(value, stage)
    return value


def exchange_gather(piece, stages):
    for stage in stages:
        piece = jnp.stack([piece, swap(piece, stage)])
    return piece


def own_places():
    return jnp.stack([lax.axis_index(axis) for axis in ALL]).astype(jnp.int32)


def turned(index, stage, places):
    axis, bit = stage
    return index ^ ((places[ALL.index(axis)] >> bit) & 1)


def block_places(part, stages, places):
    return tuple(
        turned((part >> bit) & 1, (axis, bit), places) if axis == "mp" else 0
        for axis, bit in stages
    ) + (0, 0)


def row_place(row, stages, places, sizes):
    parts = {"pr": row & 1, "dm": (row >> 1) % sizes["dm"], "dh": (row >> 1) // sizes["dm"]}
    return tuple(
        0 if axis == "mp" else turned((parts[axis] >> bit) & 1, (axis, bit), places)
        for axis, bit in stages
    )


def assemble(own_half, other_half, stages):
    mp_count = lax.axis_size("mp")
    sizes = {axis: lax.axis_size(axis) for axis in DP}
    pairs = sizes["dh"] * sizes["dm"]
    dims = stages[::-1]
    rows, cols = own_half.shape[-2:]
    block = tuple(1 if axis == "mp" else 2 for axis, bit in dims) + (rows, cols)

    def kernel(places, own_ref, other_ref, out_ref):
        source = pl.program_id(0)
        for pair in range(pairs):
            place = row_place(2 * pair, dims, places, sizes)

            @pl.when(source == 0)
            def _():
                out_ref[0, pair, 0] = own_ref[place]

            @pl.when(source == 1)
            def _():
                out_ref[0, pair, 0] = other_ref[place]

    return pl.pallas_call(
        kernel,
        out_shape=jax.ShapeDtypeStruct((mp_count, pairs, 2, rows, cols), own_half.dtype),
        grid_spec=pltpu.PrefetchScalarGridSpec(
            num_scalar_prefetch=1,
            grid=(2, mp_count),
            in_specs=[
                pl.BlockSpec(
                    block,
                    lambda source, part, places: block_places(
                        jnp.where(source == 0, part, mp_count - 1), dims, places
                    ),
                ),
                pl.BlockSpec(
                    block,
                    lambda source, part, places: block_places(
                        jnp.where(source == 1, part, 0), dims, places
                    ),
                ),
            ],
            out_specs=pl.BlockSpec(
                (1, pairs, 1, rows, cols),
                lambda source, part, places: (part, 0, source ^ places[2], 0, 0),
            ),
        ),
        cost_estimate=pl.CostEstimate(
            flops=0, transcendentals=0, bytes_accessed=8 * own_half.size
        ),
        name="assemble",
    )(own_places(), own_half, other_half)


def weight_grads(lefts, right, edge, stages):
    mp_count, tok_count, cols = right.shape
    sizes = {axis: lax.axis_size(axis) for axis in DP}
    pairs = sizes["dh"] * sizes["dm"]
    dims = stages[::-1]
    width = lefts[0].shape[0]
    rows = width // (2 * pairs)
    block = tuple(1 if axis == "mp" else 2 for axis, bit in dims) + (rows, cols)
    shape = jax.ShapeDtypeStruct((2,) * len(dims) + (rows, cols), jnp.float32)

    def kernel(places, *refs):
        left_refs = refs[: len(lefts)]
        right_ref, kept_ref, sent_ref, total_ref = refs[len(lefts) :]
        right_part = right_ref[0]
        total = jnp.dot(left_refs[0][...], right_part, preferred_element_type=jnp.float32)
        if len(lefts) > 1:
            second = jnp.dot(left_refs[1][...], right_part, preferred_element_type=jnp.float32)
            column = lax.broadcasted_iota(jnp.int32, total.shape, 1)
            total = jnp.where(column < edge, total, second)
        for row in range(2 * pairs):
            total_ref[row] = total[row * rows : (row + 1) * rows]
        for pair in range(pairs):
            place = row_place(2 * pair, dims, places, sizes)
            kept_ref[place] = total_ref[2 * pair + places[2]]
            sent_ref[place] = total_ref[2 * pair + 1 - places[2]]

    spec = pl.BlockSpec(block, lambda part, places: block_places(part, dims, places))
    return pl.pallas_call(
        kernel,
        out_shape=(shape, shape),
        grid_spec=pltpu.PrefetchScalarGridSpec(
            num_scalar_prefetch=1,
            grid=(mp_count,),
            in_specs=[
                pl.BlockSpec((width, tok_count), lambda part, places: (0, 0)) for left in lefts
            ]
            + [pl.BlockSpec((1, tok_count, cols), lambda part, places: (part, 0, 0))],
            out_specs=(spec, spec),
            scratch_shapes=[pltpu.VMEM((2 * pairs, rows, cols), jnp.float32)],
        ),
        cost_estimate=pl.CostEstimate(
            flops=2 * mp_count * width * tok_count * cols,
            transcendentals=0,
            bytes_accessed=4 * mp_count * width * cols,
        ),
        name="weight_grads",
    )(own_places(), *lefts, right)


def exchange_reduce(kept, sent, stages, wide):
    total = kept + swap(sent, ("pr", 0))
    for stage in stages[::-1]:
        sent = total[1]
        if not (wide and stage[0] == "mp"):
            sent = sent.astype(jnp.bfloat16)
        total = total[0] + swap(sent, stage).astype(jnp.float32)
    return total


def slow_gather(piece):
    piece = lax.all_gather(lax.all_gather(piece, DP, axis=0, tiled=True), "mp", axis=0)
    return piece


def slow_reduce(lefts, right, edge):
    total = jnp.einsum("dt,jtn->jdn", lefts[0], right, preferred_element_type=jnp.float32)
    if len(lefts) > 1:
        second = jnp.einsum("dt,jtn->jdn", lefts[1], right, preferred_element_type=jnp.float32)
        total = jnp.concatenate([total[..., :edge], second[..., edge:]], axis=-1)
    total = lax.psum_scatter(total, "mp", scatter_dimension=0, tiled=False)
    return lax.psum_scatter(total, DP, scatter_dimension=0, tiled=True)


def attend(queries, key_rows, values):
    scores = jnp.einsum(
        "sqhd,skhd->shqk", queries, key_rows, preferred_element_type=jnp.float32
    ) * HD ** (-0.5)
    row_peak = jnp.max(scores, axis=-1, keepdims=True)
    exponent = jnp.exp(scores - row_peak)
    row_total = jnp.sum(exponent, axis=-1, keepdims=True)
    probs = (exponent / row_total).astype(jnp.bfloat16)
    attended = jnp.einsum(
        "shqk,skhd->sqhd", probs, values, preferred_element_type=jnp.float32
    ).astype(jnp.bfloat16)
    return (attended, row_peak + jnp.log(row_total))


def attend_back(queries, key_rows, values, log_total, grad_heads):
    scores = jnp.einsum(
        "sqhd,skhd->shqk", queries, key_rows, preferred_element_type=jnp.float32
    ) * HD ** (-0.5)
    probs = jnp.exp(scores - log_total)
    probs_low = probs.astype(jnp.bfloat16)
    d_values = jnp.einsum(
        "shqk,sqhd->skhd", probs_low, grad_heads, preferred_element_type=jnp.float32
    )
    d_probs = jnp.einsum("sqhd,skhd->shqk", grad_heads, values, preferred_element_type=jnp.float32)
    d_scores = (probs * (d_probs - jnp.sum(d_probs * probs, axis=-1, keepdims=True))).astype(
        jnp.bfloat16
    )
    d_queries = jnp.einsum(
        "shqk,skhd->sqhd", d_scores, key_rows, preferred_element_type=jnp.float32
    ) * HD ** (-0.5)
    d_keys = jnp.einsum(
        "shqk,sqhd->skhd", d_scores, queries, preferred_element_type=jnp.float32
    ) * HD ** (-0.5)
    return (
        d_queries.astype(jnp.bfloat16),
        d_keys.astype(jnp.bfloat16),
        d_values.astype(jnp.bfloat16),
    )


def head_split(qkv):
    seq_count, tok_count, parts, width = qkv.shape
    third = width // 3
    return [
        qkv[..., slot * third : (slot + 1) * third].reshape(
            seq_count, tok_count, parts * third // HD, HD
        )
        for slot in range(3)
    ]


def layer_forward(stream, layer_weights, layer_mods):
    w_qkv, w_out, w_up, w_down = layer_weights
    shift_a, scale_a, gate_a, shift_b, scale_b, gate_b = [
        layer_mods[:, slot, None, :] for slot in range(6)
    ]
    seq_count, tok_count = stream.shape[:2]
    normed_a, inv_a = layer_norm(stream)
    in_a = (normed_a * (1.0 + scale_a) + shift_a).astype(jnp.bfloat16)
    qkv = jnp.einsum("std,jdn->stjn", in_a, w_qkv, preferred_element_type=jnp.float32).astype(
        jnp.bfloat16
    )
    heads = head_split(qkv)
    attended, log_total = attend(*heads)
    attended = attended.reshape(seq_count, tok_count, w_out.shape[0], w_out.shape[2])
    branch_a = jnp.einsum("stjm,jdm->std", attended, w_out, preferred_element_type=jnp.float32)
    stream_mid = stream + gate_a * branch_a
    normed_b, inv_b = layer_norm(stream_mid)
    in_b = (normed_b * (1.0 + scale_b) + shift_b).astype(jnp.bfloat16)
    hidden_pre = jnp.einsum("std,jdf->stjf", in_b, w_up, preferred_element_type=jnp.float32)
    hidden = jax.nn.gelu(hidden_pre, approximate=True).astype(jnp.bfloat16)
    branch_b = jnp.einsum("stjf,jdf->std", hidden, w_down, preferred_element_type=jnp.float32)
    saved_layer = (
        normed_a,
        inv_a,
        in_a,
        heads,
        log_total,
        attended,
        branch_a,
        normed_b,
        inv_b,
        in_b,
        hidden_pre,
        hidden,
        branch_b,
    )
    return (stream_mid + gate_b * branch_b, saved_layer)


def layer_backward(gradient, saved_layer, layer_weights, layer_mods):
    w_qkv, w_out, w_up, w_down = layer_weights
    (
        normed_a,
        inv_a,
        in_a,
        heads,
        log_total,
        attended,
        branch_a,
        normed_b,
        inv_b,
        in_b,
        hidden_pre,
        hidden,
        branch_b,
    ) = saved_layer
    shift_a, scale_a, gate_a, shift_b, scale_b, gate_b = [
        layer_mods[:, slot, None, :] for slot in range(6)
    ]
    seq_count, tok_count = gradient.shape[:2]
    low = jnp.bfloat16
    d_branch_b = (gate_b * gradient).astype(low)
    d_gate_b = jnp.sum(gradient * branch_b, axis=1)
    d_hidden = jnp.einsum("std,jdf->stjf", d_branch_b, w_down, preferred_element_type=jnp.float32)
    d_pre = jax.vjp(lambda value_in: jax.nn.gelu(value_in, approximate=True), hidden_pre)[1](
        d_hidden
    )[0].astype(low)
    d_in_b = jnp.einsum("stjf,jdf->std", d_pre, w_up, preferred_element_type=jnp.float32)
    d_scale_b = jnp.sum(d_in_b * normed_b, axis=1)
    d_shift_b = jnp.sum(d_in_b, axis=1)
    d_mid = gradient + norm_back(normed_b, inv_b, d_in_b * (1.0 + scale_b))
    d_branch_a = (gate_a * d_mid).astype(low)
    d_gate_a = jnp.sum(d_mid * branch_a, axis=1)
    d_attended = jnp.einsum(
        "std,jdm->stjm", d_branch_a, w_out, preferred_element_type=jnp.float32
    ).astype(low)
    parts = w_out.shape[0]
    d_heads = attend_back(*heads, log_total, d_attended.reshape(heads[0].shape))
    d_qkv = jnp.concatenate(
        [piece.reshape(seq_count, tok_count, parts, -1) for piece in d_heads], axis=-1
    )
    d_in_a = jnp.einsum("stjn,jdn->std", d_qkv, w_qkv, preferred_element_type=jnp.float32)
    d_scale_a = jnp.sum(d_in_a * normed_a, axis=1)
    d_shift_a = jnp.sum(d_in_a, axis=1)
    grad_in = d_mid + norm_back(normed_a, inv_a, d_in_a * (1.0 + scale_a))
    d_mods = jnp.stack([d_shift_a, d_scale_a, d_gate_a, d_shift_b, d_scale_b, d_gate_b], axis=1)

    def flat(value):
        return value.reshape((seq_count * tok_count,) + value.shape[2:])

    def parted(value):
        return flat(value).transpose(1, 0, 2)

    factors = (
        ((flat(in_b).T,), parted(d_pre)),
        ((flat(d_branch_b).T,), parted(hidden)),
        (
            (flat(in_a).T, flat(d_branch_a).T),
            parted(jnp.concatenate([d_qkv, attended], axis=-1)),
        ),
    )
    return (grad_in, d_mods, factors)


def polar_factor(gram):
    width = gram.shape[0]
    eye = jnp.eye(width, dtype=jnp.float32)
    frobenius = jnp.sqrt(jnp.trace(gram)) + 1e-07
    square = gram / (frobenius * frobenius)
    total = None
    for iteration in range(NS_ITERS):
        poly = ns_a * eye + ns_b * square + ns_c * mat_dot(square, square)
        total = poly if total is None else mat_dot(poly, total)
        if iteration < NS_ITERS - 1:
            square = mat_dot(mat_dot(poly, square), poly)
    return total / frobenius


def mat_dot(left, right):
    return jnp.dot(left, right, precision=lax.Precision.HIGH)


def adam_update(weight, gradient, first, second, rate, step_value):
    first_new = beta_one * first + (1.0 - beta_one) * gradient
    second_new = beta_two * second + (1.0 - beta_two) * gradient * gradient
    first_hat = first_new / (1.0 - jnp.power(beta_one, step_value))
    second_hat = second_new / (1.0 - jnp.power(beta_two, step_value))
    updated = weight * (1.0 - rate * adam_decay) - rate * first_hat / (
        jnp.sqrt(second_hat) + adam_eps
    )
    return (updated, first_new, second_new)


def body(
    latents,
    noise,
    labels,
    time_index,
    tables,
    time_proj,
    modulation,
    qkv_proj,
    out_proj,
    up_proj,
    down_proj,
    qkv_momentum,
    out_momentum,
    up_momentum,
    down_momentum,
    tables_first,
    tables_second,
    time_first,
    time_second,
    mod_first,
    mod_second,
    adam_step,
):
    low = jnp.bfloat16
    mp_count = lax.axis_size("mp")
    dp_count = lax.axis_size(DP)
    mp_own = lax.axis_index("mp")
    dp_own = lax.axis_index(DP)
    row_count = qkv_proj.shape[1]
    width_qkv = 3 * qkv_proj.shape[3]
    width_out = out_proj.shape[1]
    dp_stages = axis_bits("dh") + axis_bits("dm") + axis_bits("pr")
    mp_stages = axis_bits("mp")
    order = mp_stages + dp_stages
    fast = row_count % 16 == 0
    y_stages, x_stages = (axis_bits("dh"), axis_bits("dm")[::-1])
    routes = [
        [
            mp_stages + y_stages + x_stages,
            first + mp_stages + last,
            mp_stages + x_stages + y_stages,
        ]
        for first, last in ((x_stages, y_stages), (y_stages, x_stages))
    ]
    assert LAYERS == len(routes)

    def gather_whole(piece, stages):
        if not fast:
            return slow_gather(piece)
        piece = exchange_gather(piece, stages)
        return assemble(piece, swap(piece, ("pr", 0)), stages)

    def reduce_whole(lefts, right, stages, wide):
        if not fast:
            return slow_reduce(lefts, right, width_qkv)
        kept, sent = weight_grads(lefts, right, width_qkv, stages)
        return exchange_reduce(kept, sent, stages, wide)

    def oriented(qkv, out, up, down):
        layers = []
        for layer_index in range(LAYERS):
            layers.append(
                (
                    up[layer_index],
                    down[layer_index].T,
                    jnp.concatenate(
                        [qkv[layer_index].reshape(row_count, width_qkv), out[layer_index].T], axis=1
                    ),
                )
            )
        return layers

    def restored(layers):
        up = jnp.stack([pieces[0] for pieces in layers])
        down = jnp.stack([pieces[1].T for pieces in layers])
        qkv = jnp.stack(
            [pieces[2][:, :width_qkv].reshape(row_count, 3, width_qkv // 3) for pieces in layers]
        )
        out = jnp.stack([pieces[2][:, width_qkv:].T for pieces in layers])
        return (qkv, out, up, down)

    gathered = []
    for pieces in oriented(
        qkv_proj.astype(low), out_proj.astype(low), up_proj.astype(low), down_proj.astype(low)
    ):
        up_all, down_all, rest_all = [
            gather_whole(piece, stages).reshape(mp_count, dp_count * row_count, piece.shape[1])
            for piece, stages in zip(pieces, routes[len(gathered)])
        ]
        gathered.append(
            (rest_all[..., :width_qkv], rest_all[..., width_qkv:], up_all, down_all)
        )

    tables_low = tables.astype(low)
    time_low = time_proj.astype(low)
    mod_low = modulation.astype(low)
    time_in = tables_low[PATCH_IN : PATCH_IN + FREQ]
    class_table = tables_low[PATCH_IN + FREQ : PATCH_IN + FREQ + CLASSES]
    ends = jnp.concatenate([tables_low[:PATCH_IN], tables_low[PATCH_IN + FREQ + CLASSES :]], axis=0)
    index_rows = lax.all_gather(jnp.stack([labels, time_index]), DP, axis=1, tiled=True)
    every_label, every_time = (index_rows[0], index_rows[1])
    ends_all = lax.all_gather(ends, DP, axis=1, tiled=True)
    patch_w, head_t = (ends_all[:PATCH_IN], ends_all[PATCH_IN:])
    every_count = every_time.shape[0]
    freq = freq_table(every_time).astype(low)
    time_pre = jnp.dot(freq, time_in, preferred_element_type=jnp.float32)
    time_act = jax.nn.silu(time_pre).astype(low)
    onehot = (every_label[:, None] == jnp.arange(CLASSES)[None, :]).astype(low)
    time_part = jnp.dot(time_act, time_low, preferred_element_type=jnp.float32)
    time_part = time_part.reshape(every_count, dp_count, row_count).transpose(1, 0, 2)
    time_part = lax.all_to_all(time_part, DP, split_axis=0, concat_axis=0, tiled=True)
    condition = jnp.sum(time_part, axis=0) + jnp.dot(
        onehot, class_table, preferred_element_type=jnp.float32
    )
    cond_act = jax.nn.silu(condition).astype(low)
    mod_part = jnp.dot(cond_act, mod_low, preferred_element_type=jnp.float32)
    seq_count = every_count // (dp_count * mp_count)
    mod_width = mod_low.shape[1]
    mod_part = lax.all_to_all(mod_part, ALL, split_axis=0, concat_axis=0, tiled=True)
    mod_rows = jnp.sum(mod_part.reshape(dp_count, mp_count, seq_count, mod_width), axis=0)
    mod_rows = mod_rows.transpose(1, 0, 2).reshape(seq_count, mp_count * mod_width)

    first_row = mp_own * seq_count
    latent_rows = lax.dynamic_slice_in_dim(latents, first_row, seq_count, 0)
    noise_rows = lax.dynamic_slice_in_dim(noise, first_row, seq_count, 0)
    time_rows = lax.dynamic_slice_in_dim(time_index, first_row, seq_count, 0)
    token_count = every_count * TOK * PATCH_IN
    times = ((time_rows.astype(jnp.float32) + 0.5) / TSTEPS)[:, None, None]
    latents_f = latent_rows.astype(jnp.float32)
    noise_f = noise_rows.astype(jnp.float32)
    noisy = ((1.0 - times) * latents_f + times * noise_f).astype(low)
    target = noise_f - latents_f
    stream = (
        jnp.einsum("stp,pd->std", noisy, patch_w, preferred_element_type=jnp.float32)
        + position_table()[None]
    )
    layer_mods = [
        mod_rows[:, layer_index * 6 * D : (layer_index + 1) * 6 * D].reshape(seq_count, 6, D)
        for layer_index in range(LAYERS)
    ]
    saved_all = []
    for layer_index in range(LAYERS):
        stream, saved_layer = layer_forward(stream, gathered[layer_index], layer_mods[layer_index])
        saved_all.append(saved_layer)
    base = 6 * LAYERS * D
    shift_f = mod_rows[:, None, base : base + D]
    scale_f = mod_rows[:, None, base + D : base + 2 * D]
    normed_f, inv_f = layer_norm(stream)
    in_f = (normed_f * (1.0 + scale_f) + shift_f).astype(low)
    output = jnp.einsum("std,pd->stp", in_f, head_t, preferred_element_type=jnp.float32)
    weight_t = 0.5 + times
    velocity_miss = output - target
    loss_part = jnp.sum(weight_t * velocity_miss * velocity_miss) / token_count
    d_output = (2.0 * weight_t * velocity_miss / token_count).astype(low)
    d_head = jnp.einsum("stp,std->pd", d_output, in_f, preferred_element_type=jnp.float32)
    d_in_f = jnp.einsum("stp,pd->std", d_output, head_t, preferred_element_type=jnp.float32)
    d_scale_f = jnp.sum(d_in_f * normed_f, axis=1)
    d_shift_f = jnp.sum(d_in_f, axis=1)
    gradient = norm_back(normed_f, inv_f, d_in_f * (1.0 + scale_f))
    mod_grads = [None] * LAYERS
    layer_grads = [None] * LAYERS
    for layer_index in reversed(range(LAYERS)):
        gradient, d_mods, factors = layer_backward(
            gradient, saved_all[layer_index], gathered[layer_index], layer_mods[layer_index]
        )
        mod_grads[layer_index] = d_mods.reshape(seq_count, 6 * D)
        layer_grads[layer_index] = [
            reduce_whole(lefts, right, stages, len(lefts) > 1)
            for (lefts, right), stages in zip(factors, routes[layer_index])
        ]
    d_first = gradient.astype(low)
    d_patch = jnp.einsum("stp,std->pd", noisy, d_first, preferred_element_type=jnp.float32)
    d_ends = exchange_sum(jnp.concatenate([d_patch, d_head], axis=0), order[::-1])
    d_ends = lax.dynamic_slice_in_dim(d_ends, dp_own * row_count, row_count, 1)
    d_mod_all = jnp.concatenate(mod_grads + [d_shift_f, d_scale_f], axis=1).astype(low)
    d_mod_all = d_mod_all.reshape(seq_count, mp_count, mod_width).transpose(1, 0, 2)
    d_mod_sent = jnp.broadcast_to(
        d_mod_all[None], (dp_count, mp_count, seq_count, mod_width)
    ).reshape(every_count, mod_width)
    d_mod_own = lax.all_to_all(d_mod_sent, ALL, split_axis=0, concat_axis=0, tiled=True)
    grad_mod = jnp.einsum("sd,sm->dm", cond_act, d_mod_own, preferred_element_type=jnp.float32)
    d_cond_act = exchange_sum(
        jnp.einsum("sm,dm->sd", d_mod_own, mod_low, preferred_element_type=jnp.float32), mp_stages
    )
    d_condition = jax.vjp(jax.nn.silu, condition)[1](d_cond_act)[0].astype(low)
    d_class = jnp.einsum("sc,sd->cd", onehot, d_condition, preferred_element_type=jnp.float32)
    d_condition_all = lax.all_gather(d_condition, DP, axis=1, tiled=True)
    grad_time = jnp.einsum("se,sd->ed", time_act, d_condition_all, preferred_element_type=jnp.float32)
    d_time_act = jnp.einsum(
        "sd,ed->se", d_condition_all, time_low, preferred_element_type=jnp.float32
    )
    d_time_pre = jax.vjp(jax.nn.silu, time_pre)[1](d_time_act)[0].astype(low)
    d_time_in = jnp.einsum("sf,sd->fd", freq, d_time_pre, preferred_element_type=jnp.float32)
    grad_tables = jnp.concatenate(
        [d_ends[:PATCH_IN], d_time_in, d_class, d_ends[PATCH_IN:]], axis=0
    )

    shared_square = (jnp.sum(grad_tables * grad_tables) + jnp.sum(grad_time * grad_time)) / mp_count
    own_square = jnp.sum(grad_mod * grad_mod) + sum(
        jnp.sum(piece * piece) for pieces in layer_grads for piece in pieces
    )
    scalars = jnp.stack([shared_square + own_square, loss_part])
    scalars = jnp.broadcast_to(jnp.pad(scalars, (0, 126))[None], (8, 128))
    scalars = exchange_sum(scalars, order[::-1])
    square_total, loss = (scalars[0, 0], scalars[0, 1])
    grad_norm = jnp.sqrt(square_total)
    factor = jnp.minimum(1.0, clip_norm / (grad_norm + 1e-06))
    step_value = adam_step[0].astype(jnp.float32)
    tables_updated, tables_first_new, tables_second_new = adam_update(
        tables, grad_tables * factor, tables_first, tables_second, rate_tables, step_value
    )
    time_updated, time_first_new, time_second_new = adam_update(
        time_proj, grad_time * factor, time_first, time_second, rate_time, step_value
    )
    mod_updated, mod_first_new, mod_second_new = adam_update(
        modulation, grad_mod * factor, mod_first, mod_second, rate_modulation, step_value
    )

    momenta = oriented(qkv_momentum, out_momentum, up_momentum, down_momentum)
    momenta_new = [
        [muon_mu * momentum + factor * grad for momentum, grad in zip(old, new)]
        for old, new in zip(momenta, layer_grads)
    ]
    pushes = [
        [factor * grad + muon_mu * momentum for momentum, grad in zip(new_momentum, new)]
        for new_momentum, new in zip(momenta_new, layer_grads)
    ]
    group = dp_count // 2
    piece_cols = up_proj.shape[2] // group

    def cut(matrix):
        pieces = matrix.reshape(row_count, group, matrix.shape[1] // group)
        pieces = pieces.transpose(1, 0, 2)
        return jnp.pad(pieces, ((0, 0), (0, 0), (0, piece_cols - pieces.shape[2])))

    sent = []
    for up, down, rest in pushes:
        sent += [cut(up), cut(down), cut(rest[:, :width_qkv]), cut(rest[:, width_qkv:])]
    sent = jnp.stack(sent).reshape(dp_count * mp_count, row_count, piece_cols)
    got = lax.all_to_all(sent, MATS, split_axis=0, concat_axis=0, tiled=True)
    got = got.reshape(2, mp_count, group, row_count, piece_cols).transpose(0, 2, 3, 1, 4)
    matrix = got.reshape(2 * group * row_count, mp_count * piece_cols)
    gram = gram_sum(mat_dot(matrix, matrix.T))
    polar = polar_factor(gram)
    ortho = mat_dot(polar, matrix).astype(low)
    ortho = ortho.reshape(2, group, row_count, mp_count, piece_cols).transpose(0, 3, 1, 2, 4)
    ortho = ortho.reshape(dp_count * mp_count, row_count, piece_cols)
    back = lax.all_to_all(ortho, MATS, split_axis=0, concat_axis=0, tiled=True)
    back = back.reshape(4 * LAYERS, group, row_count, piece_cols)

    def joined(slot, width):
        pieces = back[slot][:, :, : width // group].transpose(1, 0, 2)
        return pieces.reshape(row_count, width).astype(jnp.float32)

    down_scale = math.sqrt(max(1.0, FF / D))
    ortho_layers = [
        (
            joined(4 * layer_index, up_proj.shape[2]),
            down_scale * joined(4 * layer_index + 1, up_proj.shape[2]),
            jnp.concatenate(
                [
                    joined(4 * layer_index + 2, width_qkv),
                    joined(4 * layer_index + 3, width_out),
                ],
                axis=1,
            ),
        )
        for layer_index in range(LAYERS)
    ]
    keep_factor = 1.0 - muon_rate * muon_decay
    updated = [
        weight * keep_factor - muon_rate * push
        for weight, push in zip((qkv_proj, out_proj, up_proj, down_proj), restored(ortho_layers))
    ]
    momenta_out = restored(momenta_new)
    return (
        loss,
        grad_norm,
        updated[0],
        momenta_out[0],
        updated[1],
        momenta_out[1],
        updated[2],
        momenta_out[2],
        updated[3],
        momenta_out[3],
        tables_updated,
        tables_first_new,
        tables_second_new,
        time_updated,
        time_first_new,
        time_second_new,
        mod_updated,
        mod_first_new,
        mod_second_new,
    )


def gram_sum(partial):
    half = partial.shape[0] // 2
    mine = lax.axis_index("pr")
    sent = lax.dynamic_slice_in_dim(partial, (1 - mine) * half, half, 0)
    kept = lax.dynamic_slice_in_dim(partial, mine * half, half, 0)
    kept = kept + swap(sent, ("pr", 0))
    kept = exchange_sum(kept, axis_bits("dm"))
    other_half = swap(kept, ("pr", 0))
    upper = mine == 1
    return jnp.concatenate(
        [jnp.where(upper, other_half, kept), jnp.where(upper, kept, other_half)], axis=0
    )


def solution(mesh):
    shape = mesh.devices.shape
    split = Mesh(mesh.devices.reshape(2, shape[0] // 4, 2, shape[1]), ALL)
    return jax.shard_map(
        body,
        mesh=split,
        in_specs=(
            P(DP, None, None),
            P(DP, None, None),
            P(DP),
            P(DP),
            P(None, DP),
            P(DP, None),
            P(DP, "mp"),
            P(None, DP, None, "mp"),
            P(None, "mp", DP),
            P(None, DP, "mp"),
            P(None, "mp", DP),
            P(None, DP, None, "mp"),
            P(None, "mp", DP),
            P(None, DP, "mp"),
            P(None, "mp", DP),
            P(None, DP),
            P(None, DP),
            P(DP, None),
            P(DP, None),
            P(DP, "mp"),
            P(DP, "mp"),
            P(),
        ),
        out_specs=(
            P(),
            P(),
            P(None, DP, None, "mp"),
            P(None, DP, None, "mp"),
            P(None, "mp", DP),
            P(None, "mp", DP),
            P(None, DP, "mp"),
            P(None, DP, "mp"),
            P(None, "mp", DP),
            P(None, "mp", DP),
            P(None, DP),
            P(None, DP),
            P(None, DP),
            P(DP, None),
            P(DP, None),
            P(DP, None),
            P(DP, "mp"),
            P(DP, "mp"),
            P(DP, "mp"),
        ),
        check_vma=False,
    )
```

time: 2530 us -> 1020 us (0.40)
  waiting for transfers between devices: 1830 us -> 354 us
  local copies, waits for them, and re-layouts: 221 us -> 119 us
  Pallas kernels: 0 us -> 95.3 us
  starting transfers between devices: 7.45 us -> 90.1 us
  matrix products: 233 us -> 158 us
  blocking collectives: 96.7 us -> 28.4 us
  other arithmetic: 103 us -> 150 us
    psum x13 -> x0, waiting for transfers between devices: 1300 us -> none  [the longest x5 470 us: gram_product(): return lax.psum(jnp.dot(matrix, matrix.T, precision=highest), 'mp')]
    ppermute x0 -> x75, waiting for transfers between devices: none -> 256 us  [swap(): lax.ppermute(value, axis, [(place, place ^ 1 << bit) for place in range(l...]
    unnamed x30 -> x0, waiting for transfers between devices: 220 us -> none
    all_gather x7 -> x0, waiting for transfers between devices: 202 us -> none  [the longest x1 99.6 us: body(): everything = lax.all_gather(stacked, 'dp', axis=1, tiled=True)]
    unnamed x841 -> x411, local copies, waits for them, and re-layouts: 163 us -> 44.8 us
    reduce_scatter x2 -> x0, waiting for transfers between devices: 114 us -> none  [the longest x1 71 us: body(): lax.psum_scatter(grad_sums[2], 'dp', scatter_dimension=0, tiled=True)]
    all_to_all x1 -> x5, waiting for transfers between devices: 0.01 us -> 97.7 us  [the longest x1 72.4 us: body(): got = lax.all_to_all(sent, MATS, split_axis=0, concat_axis=0, tiled=True)]
    pallas_call x0 -> x12, Pallas kernels: none -> 95.3 us  [the longest x6 49.9 us: assemble(): pl.pallas_call(kernel, out_shape=jax.ShapeDtypeStruct((mp_count, pairs, 2...]
  transfers between devices with their start and end apart: 27 -> 80, of which waited for: 25 -> 36; matrix products, arithmetic and copies ran while one was open for 10% -> 20% of each run, Pallas kernels for 0% -> 8%
where the time goes in v1:
time: 1020 us; the launch traced here: 1010 us
  waiting for transfers between devices  354 us (35%)
  matrix products  158 us (15%)
  other arithmetic  150 us (15%)
  local copies, waits for them, and re-layouts  119 us (12%)
  Pallas kernels  95.3 us (9%)
  starting transfers between devices  90.1 us (9%)
  blocking collectives  28.4 us (3%)
  between operations  14.4 us (1%)
    ppermute x75, waiting for transfers between devices, swap(): lax.ppermute(value, axis, [(place, place ^ 1 << bit) for place in range(l...  256 us
    all_to_all x1, waiting for transfers between devices, body(): got = lax.all_to_all(sent, MATS, split_axis=0, concat_axis=0, tiled=True)  72.4 us
    ppermute x75, starting transfers between devices, swap(): lax.ppermute(value, axis, [(place, place ^ 1 << bit) for place in range(l...  71.6 us
    dot_general x19, matrix products, mat_dot(): return jnp.dot(left, right, precision=lax.Precision.HIGH)  65 us
    pallas_call x6, Pallas kernels, assemble(): pl.pallas_call(kernel, out_shape=jax.ShapeDtypeStruct((mp_count, pairs, 2...  49.9 us
    pallas_call x6, Pallas kernels, weight_grads(): pl.pallas_call(kernel, out_shape=(shape, shape), grid_spec=pltpu.Prefetch...  45.4 us
    unnamed x411, local copies, waits for them, and re-layouts  44.8 us
    another operation x26, other arithmetic, exchange_gather(): piece = jnp.stack([piece, swap(piece, stage)])  37.6 us
  transfers between devices with their start and end apart: 80, of which 36 were waited for; matrix products, arithmetic and copies ran while one was open for 20% of the time, Pallas kernels for 8%

profile of v1, /device:TPU:0, one launch (start us, length us, event | category | flops | bytes accessed | tf_op | source)
XLA Modules:
  0.0 1009.0 jit_solution(18353826119727450517)
XLA Ops:
  2.8 10.4 %all-gather.1 = s32[8,4,2]{1,2,0:T(2,128)S(1)} all-gather(s32[1,4,2]{1,2,0:T(2,128)S(1)} %add_bitcast_fusion), channel_id=1, replica_groups=mesh['dh'=2,'dm'=2,'pr'=2,'mp'=4] {'dh','dm','pr'}, dimensions={0}, use_global_device_ids=true | all-gather | bytes 288 | tf_op jit(solution)/shard_map/all_gather | solution.py:539
  35.1 8.3 all-gather
  97.9 8.2 collective-permute-done.12
  140.6 12.2 %collective-permute-done.22 = bf16[2,2,96,768]{3,2,1,0:T(8,128)(2,1)} collective-permute-done((bf16[2,2,96,768]{3,2,1,0:T(8,128)(2,1)}, bf16[2,2,96,768]{3,2,1,0:T(8,128)(2,1)}, u32[]{:S(2)}, u32[]{:S(2)}) %collective-permute-start.22) | collective-permute-done | bytes 589856 | tf_op jit(solution)/shard_map/ppermute | solution.py:88
  166.2 11.4 %collective-permute-done.18 = bf16[2,2,2,96,768]{4,3,2,1,0:T(8,128)(2,1)} collective-permute-done((bf16[2,2,2,96,768]{4,3,2,1,0:T(8,128)(2,1)}, bf16[2,2,2,96,768]{4,3,2,1,0:T(8,128)(2,1)}, u32[]{:S(2)}, u32[]{:S(2)}) %collective-permute-start.18) | collective-permute-done | bytes 1179680 | tf_op jit(solution)/shard_map/ppermute | solution.py:88
  185.0 19.5 %collective-permute-done.23 = bf16[2,2,2,96,768]{4,3,2,1,0:T(8,128)(2,1)} collective-permute-done((bf16[2,2,2,96,768]{4,3,2,1,0:T(8,128)(2,1)}, bf16[2,2,2,96,768]{4,3,2,1,0:T(8,128)(2,1)}, u32[]{:S(2)}, u32[]{:S(2)}) %collective-permute-start.23) | collective-permute-done | bytes 1179680 | tf_op jit(solution)/shard_map/ppermute | solution.py:88
  207.9 8.2 assemble.6
  221.1 8.2 assemble.7
  240.2 8.2 assemble.9
  251.7 8.5 assemble.8
  274.1 8.3 assemble.10
  293.4 8.4 assemble.11
  442.8 8.1 weight_grads.8
  491.7 8.1 weight_grads.11
  502.5 9.7 all-gather.2
  560.1 22.2 %collective-permute-done.48 = bf16[2,2,2,96,768]{4,3,2,1,0:T(8,128)(2,1)} collective-permute-done((bf16[2,2,2,96,768]{4,3,2,1,0:T(8,128)(2,1)}, bf16[2,2,2,96,768]{4,3,2,1,0:T(8,128)(2,1)}, u32[]{:S(2)}, u32[]{:S(2)}) %collective-permute-start.48) | collective-permute-done | bytes 1179680 | tf_op jit(solution)/shard_map/ppermute | solution.py:88
  588.6 14.1 %collective-permute-done.58 = bf16[2,2,2,96,768]{4,3,2,1,0:T(8,128)(2,1)} collective-permute-done((bf16[2,2,2,96,768]{4,3,2,1,0:T(8,128)(2,1)}, bf16[2,2,2,96,768]{4,3,2,1,0:T(8,128)(2,1)}, u32[]{:S(2)}, u32[]{:S(2)}) %collective-permute-start.58) | collective-permute-done | bytes 1179680 | tf_op jit(solution)/shard_map/ppermute | solution.py:88
  609.4 10.7 %collective-permute-done.39 = bf16[2,2,96,768]{3,2,1,0:T(8,128)(2,1)S(1)} collective-permute-done((bf16[2,2,96,768]{3,2,1,0:T(8,128)(2,1)S(1)}, bf16[2,2,96,768]{3,2,1,0:T(8,128)(2,1)S(1)}, u32[]{:S(2)}, u32[]{:S(2)}) %collective-permute-start.39) | collective-permute-done | bytes 589856 | tf_op jit(solution)/shard_map/ppermute | solution.py:88
  639.3 25.6 %collective-permute-done.55 = bf16[2,96,768]{2,1,0:T(8,128)(2,1)S(1)} collective-permute-done((bf16[2,96,768]{2,1,0:T(8,128)(2,1)S(1)}, bf16[2,96,768]{2,1,0:T(8,128)(2,1)S(1)}, u32[]{:S(2)}, u32[]{:S(2)}) %collective-permute-start.55) | collective-permute-done | bytes 294944 | tf_op jit(solution)/shard_map/ppermute | solution.py:88
  667.4 9.3 collective-permute-done.41
  687.6 13.5 %collective-permute-done.51 = f32[96,768]{1,0:T(8,128)S(1)} collective-permute-done((f32[96,768]{1,0:T(8,128)}, f32[96,768]{1,0:T(8,128)S(1)}, u32[]{:S(2)}, u32[]{:S(2)}) %collective-permute-start.51) | collective-permute-done | bytes 294944 | tf_op jit(solution)/shard_map/ppermute | solution.py:88
  758.2 72.4 %all-to-all-done.3 = f32[32,96,192]{2,1,0:T(8,128)S(1)} async-done(((f32[32,96,192]{2,1,0:T(8,128)}), f32[32,96,192]{2,1,0:T(8,128)S(1)}, u32[]{:S(2)}, u32[]{:S(2)}) %all-to-all-start.3) | async-done | bytes 2359328 | tf_op jit(solution)/shard_map/all_to_all | solution.py:679
  848.7 26.8 %collective-permute-done.73 = f32[384,768]{1,0:T(8,128)S(1)} collective-permute-done((f32[384,768]{1,0:T(8,128)S(1)}, f32[384,768]{1,0:T(8,128)S(1)}, u32[]{:S(2)}, u32[]{:S(2)}) %collective-permute-start.73) | collective-permute-done | bytes 1179680 | tf_op jit(solution)/shard_map/ppermute | solution.py:88
  976.3 25.3 %all-to-all-done.4 = bf16[32,96,192]{2,1,0:T(8,128)(2,1)S(1)} async-done(((bf16[32,96,192]{2,1,0:T(8,128)(2,1)}), bf16[32,96,192]{2,1,0:T(8,128)(2,1)S(1)}, u32[]{:S(2)}, u32[]{:S(2)}) %all-to-all-start.4) | async-done | bytes 1179680 | tf_op jit(solution)/shard_map/all_to_all | solution.py:687
  (923 shorter events, 628.9 us)
Async XLA Ops:
  16.6 45.6 %all-to-all-start = ((f32[8,32,96]{2,1,0:T(8,128)}), f32[8,32,96]{2,1,0:T(8,128)S(1)}, u32[]{:S(2)}, u32[]{:S(2)}) async-start(f32[8,32,96]{2,1,0:T(8,128)} %bitcast.747), calls=%async_computation | async-start | bytes 262144 | tf_op jit(solution)/shard_map/all_to_all | solution.py:550
  32.3 58.2 %collective-permute-start.25 = (bf16[96,768]{1,0:T(8,128)(2,1)}, bf16[96,768]{1,0:T(8,128)(2,1)}, u32[]{:S(2)}, u32[]{:S(2)}) collective-permute-start(bf16[96,768]{1,0:T(8,128)(2,1)} %get-tuple-element.275), channel_id=1, source_target_pairs={{0,16},{16,0},{1,17},{17,1},{2,18},{18,2},{3,19},{19,3},{4,20},{20... | collective-permute-start | bytes 442376 | tf_op jit(solution)/shard_map/ppermute | solution.py:88
  107.8 48.7 %collective-permute-start.13 = (bf16[2,2,2,96,768]{4,3,2,1,0:T(8,128)(2,1)}, bf16[2,2,2,96,768]{4,3,2,1,0:T(8,128)(2,1)}, u32[]{:S(2)}, u32[]{:S(2)}) collective-permute-start(bf16[2,2,2,96,768]{4,3,2,1,0:T(8,128)(2,1)} %get-tuple-element.232), channel_id=1, source_target_pairs={{0,16},{16,0},{1,17},{17,1},{2,18},{18,2},{3,19},{19,3},{4,20},{20... | collective-permute-start | bytes 3538952 | tf_op jit(solution)/shard_map/ppermute | solution.py:88
  116.0 91.4 %collective-permute-start.4 = (bf16[2,2,2,2,96,768]{5,4,3,2,1,0:T(8,128)(2,1)S(1)}, bf16[2,2,2,2,96,768]{5,4,3,2,1,0:T(8,128)(2,1)}, u32[]{:S(2)}, u32[]{:S(2)}) collective-permute-start(bf16[2,2,2,2,96,768]{5,4,3,2,1,0:T(8,128)(2,1)S(1)} %pad_maximum_fusion.own_ref), channel_id=1, source_target_pairs={{0,4},{4,0},{1,5},{5,1},{2,6},{6,2},{3,7},{7,3},{8,12},{12,8},{9,1... | collective-permute-start | bytes 7077896 | tf_op jit(solution)/shard_map/ppermute | solution.py:88
  133.0 44.6 %collective-permute-start.18 = (bf16[2,2,2,96,768]{4,3,2,1,0:T(8,128)(2,1)}, bf16[2,2,2,96,768]{4,3,2,1,0:T(8,128)(2,1)}, u32[]{:S(2)}, u32[]{:S(2)}) collective-permute-start(bf16[2,2,2,96,768]{4,3,2,1,0:T(8,128)(2,1)} %get-tuple-element.228), channel_id=1, source_target_pairs={{0,16},{16,0},{1,17},{17,1},{2,18},{18,2},{3,19},{19,3},{4,20},{20... | collective-permute-start | bytes 3538952 | tf_op jit(solution)/shard_map/ppermute | solution.py:88
  137.9 83.2 %collective-permute-start.9 = (bf16[2,2,2,2,96,768]{5,4,3,2,1,0:T(8,128)(2,1)}, bf16[2,2,2,2,96,768]{5,4,3,2,1,0:T(8,128)(2,1)}, u32[]{:S(2)}, u32[]{:S(2)}) collective-permute-start(bf16[2,2,2,2,96,768]{5,4,3,2,1,0:T(8,128)(2,1)} %pad_maximum_fusion.1.own_ref), channel_id=1, source_target_pairs={{0,4},{4,0},{1,5},{5,1},{2,6},{6,2},{3,7},{7,3},{8,12},{12,8},{9,1... | collective-permute-start | bytes 7077896 | tf_op jit(solution)/shard_map/ppermute | solution.py:88
  156.5 48.0 %collective-permute-start.23 = (bf16[2,2,2,96,768]{4,3,2,1,0:T(8,128)(2,1)}, bf16[2,2,2,96,768]{4,3,2,1,0:T(8,128)(2,1)}, u32[]{:S(2)}, u32[]{:S(2)}) collective-permute-start(bf16[2,2,2,96,768]{4,3,2,1,0:T(8,128)(2,1)} %get-tuple-element.221), channel_id=1, source_target_pairs={{0,8},{8,0},{1,9},{9,1},{2,10},{10,2},{3,11},{11,3},{4,12},{12,4},... | collective-permute-start | bytes 3538952 | tf_op jit(solution)/shard_map/ppermute | solution.py:88
  177.6 74.1 %collective-permute-start.14 = (bf16[2,2,2,2,96,768]{5,4,3,2,1,0:T(8,128)(2,1)}, bf16[2,2,2,2,96,768]{5,4,3,2,1,0:T(8,128)(2,1)}, u32[]{:S(2)}, u32[]{:S(2)}) collective-permute-start(bf16[2,2,2,2,96,768]{5,4,3,2,1,0:T(8,128)(2,1)} %pad_maximum_fusion.2.own_ref), channel_id=1, source_target_pairs={{0,4},{4,0},{1,5},{5,1},{2,6},{6,2},{3,7},{7,3},{8,12},{12,8},{9,1... | collective-permute-start | bytes 7077896 | tf_op jit(solution)/shard_map/ppermute | solution.py:88
  182.0 58.2 %collective-permute-start.19 = (bf16[2,2,2,2,96,768]{5,4,3,2,1,0:T(8,128)(2,1)}, bf16[2,2,2,2,96,768]{5,4,3,2,1,0:T(8,128)(2,1)}, u32[]{:S(2)}, u32[]{:S(2)}) collective-permute-start(bf16[2,2,2,2,96,768]{5,4,3,2,1,0:T(8,128)(2,1)} %pad_maximum_fusion.3.own_ref), channel_id=1, source_target_pairs={{0,4},{4,0},{1,5},{5,1},{2,6},{6,2},{3,7},{7,3},{8,12},{12,8},{9,1... | collective-permute-start | bytes 7077896 | tf_op jit(solution)/shard_map/ppermute | solution.py:88
  204.5 88.9 %collective-permute-start.29 = (bf16[2,2,2,2,96,768]{5,4,3,2,1,0:T(8,128)(2,1)}, bf16[2,2,2,2,96,768]{5,4,3,2,1,0:T(8,128)(2,1)}, u32[]{:S(2)}, u32[]{:S(2)}) collective-permute-start(bf16[2,2,2,2,96,768]{5,4,3,2,1,0:T(8,128)(2,1)} %pad_maximum_fusion.5.own_ref), channel_id=1, source_target_pairs={{0,4},{4,0},{1,5},{5,1},{2,6},{6,2},{3,7},{7,3},{8,12},{12,8},{9,1... | collective-permute-start | bytes 7077896 | tf_op jit(solution)/shard_map/ppermute | solution.py:88
  207.4 66.7 %collective-permute-start.24 = (bf16[2,2,2,2,96,768]{5,4,3,2,1,0:T(8,128)(2,1)}, bf16[2,2,2,2,96,768]{5,4,3,2,1,0:T(8,128)(2,1)}, u32[]{:S(2)}, u32[]{:S(2)}) collective-permute-start(bf16[2,2,2,2,96,768]{5,4,3,2,1,0:T(8,128)(2,1)} %pad_maximum_fusion.4.own_ref), channel_id=1, source_target_pairs={{0,4},{4,0},{1,5},{5,1},{2,6},{6,2},{3,7},{7,3},{8,12},{12,8},{9,1... | collective-permute-start | bytes 7077896 | tf_op jit(solution)/shard_map/ppermute | solution.py:88
  401.1 98.6 %collective-permute-start.37 = (f32[2,2,2,2,96,768]{5,4,3,2,1,0:T(8,128)}, f32[2,2,2,2,96,768]{5,4,3,2,1,0:T(8,128)}, u32[]{:S(2)}, u32[]{:S(2)}) collective-permute-start(f32[2,2,2,2,96,768]{5,4,3,2,1,0:T(8,128)} %get-tuple-element.32), channel_id=1, source_target_pairs={{0,4},{4,0},{1,5},{5,1},{2,6},{6,2},{3,7},{7,3},{8,12},{12,8},{9,1... | collective-permute-start | bytes 14155784 | tf_op jit(solution)/shard_map/ppermute | solution.py:88
  440.3 82.7 %collective-permute-start.42 = (f32[2,2,2,2,96,768]{5,4,3,2,1,0:T(8,128)}, f32[2,2,2,2,96,768]{5,4,3,2,1,0:T(8,128)}, u32[]{:S(2)}, u32[]{:S(2)}) collective-permute-start(f32[2,2,2,2,96,768]{5,4,3,2,1,0:T(8,128)} %get-tuple-element.34), channel_id=1, source_target_pairs={{0,4},{4,0},{1,5},{5,1},{2,6},{6,2},{3,7},{7,3},{8,12},{12,8},{9,1... | collective-permute-start | bytes 14155784 | tf_op jit(solution)/shard_map/ppermute | solution.py:88
  450.8 77.0 %collective-permute-start.47 = (f32[2,2,2,2,96,768]{5,4,3,2,1,0:T(8,128)}, f32[2,2,2,2,96,768]{5,4,3,2,1,0:T(8,128)}, u32[]{:S(2)}, u32[]{:S(2)}) collective-permute-start(f32[2,2,2,2,96,768]{5,4,3,2,1,0:T(8,128)} %get-tuple-element.36), channel_id=1, source_target_pairs={{0,4},{4,0},{1,5},{5,1},{2,6},{6,2},{3,7},{7,3},{8,12},{12,8},{9,1... | collective-permute-start | bytes 14155784 | tf_op jit(solution)/shard_map/ppermute | solution.py:88
  460.3 73.3 %collective-permute-start.52 = (f32[2,2,2,2,96,768]{5,4,3,2,1,0:T(8,128)}, f32[2,2,2,2,96,768]{5,4,3,2,1,0:T(8,128)}, u32[]{:S(2)}, u32[]{:S(2)}) collective-permute-start(f32[2,2,2,2,96,768]{5,4,3,2,1,0:T(8,128)} %get-tuple-element.38), channel_id=1, source_target_pairs={{0,4},{4,0},{1,5},{5,1},{2,6},{6,2},{3,7},{7,3},{8,12},{12,8},{9,1... | collective-permute-start | bytes 14155784 | tf_op jit(solution)/shard_map/ppermute | solution.py:88
  488.6 49.8 %collective-permute-start.57 = (f32[2,2,2,2,96,768]{5,4,3,2,1,0:T(8,128)}, f32[2,2,2,2,96,768]{5,4,3,2,1,0:T(8,128)}, u32[]{:S(2)}, u32[]{:S(2)}) collective-permute-start(f32[2,2,2,2,96,768]{5,4,3,2,1,0:T(8,128)} %get-tuple-element.40), channel_id=1, source_target_pairs={{0,4},{4,0},{1,5},{5,1},{2,6},{6,2},{3,7},{7,3},{8,12},{12,8},{9,1... | collective-permute-start | bytes 14155784 | tf_op jit(solution)/shard_map/ppermute | solution.py:88
  533.6 48.7 %collective-permute-start.48 = (bf16[2,2,2,96,768]{4,3,2,1,0:T(8,128)(2,1)}, bf16[2,2,2,96,768]{4,3,2,1,0:T(8,128)(2,1)}, u32[]{:S(2)}, u32[]{:S(2)}) collective-permute-start(bf16[2,2,2,96,768]{4,3,2,1,0:T(8,128)(2,1)} %fusion.156), channel_id=1, source_target_pairs={{0,16},{16,0},{1,17},{17,1},{2,18},{18,2},{3,19},{19,3},{4,20},{20... | collective-permute-start | bytes 3538952 | tf_op jit(solution)/shard_map/ppermute | solution.py:88
  538.4 47.1 %collective-permute-start.53 = (bf16[2,2,2,96,768]{4,3,2,1,0:T(8,128)(2,1)}, bf16[2,2,2,96,768]{4,3,2,1,0:T(8,128)(2,1)}, u32[]{:S(2)}, u32[]{:S(2)}) collective-permute-start(bf16[2,2,2,96,768]{4,3,2,1,0:T(8,128)(2,1)} %fusion.157), channel_id=1, source_target_pairs={{0,8},{8,0},{1,9},{9,1},{2,10},{10,2},{3,11},{11,3},{4,12},{12,4},... | collective-permute-start | bytes 3538952 | tf_op jit(solution)/shard_map/ppermute | solution.py:88
  544.0 58.7 %collective-permute-start.58 = (bf16[2,2,2,96,768]{4,3,2,1,0:T(8,128)(2,1)}, bf16[2,2,2,96,768]{4,3,2,1,0:T(8,128)(2,1)}, u32[]{:S(2)}, u32[]{:S(2)}) collective-permute-start(bf16[2,2,2,96,768]{4,3,2,1,0:T(8,128)(2,1)} %fusion.158), channel_id=1, source_target_pairs={{0,8},{8,0},{1,9},{9,1},{2,10},{10,2},{3,11},{11,3},{4,12},{12,4},... | collective-permute-start | bytes 3538952 | tf_op jit(solution)/shard_map/ppermute | solution.py:88
  552.2 55.3 %collective-permute-start.63 = (bf16[2,2,2,96,768]{4,3,2,1,0:T(8,128)(2,1)S(1)}, bf16[2,2,2,96,768]{4,3,2,1,0:T(8,128)(2,1)S(1)}, u32[]{:S(2)}, u32[]{:S(2)}) collective-permute-start(bf16[2,2,2,96,768]{4,3,2,1,0:T(8,128)(2,1)S(1)} %fusion.159), channel_id=1, source_target_pairs={{0,16},{16,0},{1,17},{17,1},{2,18},{18,2},{3,19},{19,3},{4,20},{20... | collective-permute-start | bytes 3538952 | tf_op jit(solution)/shard_map/ppermute | solution.py:88
  557.0 63.1 %collective-permute-start.39 = (bf16[2,2,96,768]{3,2,1,0:T(8,128)(2,1)S(1)}, bf16[2,2,96,768]{3,2,1,0:T(8,128)(2,1)S(1)}, u32[]{:S(2)}, u32[]{:S(2)}) collective-permute-start(bf16[2,2,96,768]{3,2,1,0:T(8,128)(2,1)S(1)} %fusion.225), channel_id=1, source_target_pairs={{0,16},{16,0},{1,17},{17,1},{2,18},{18,2},{3,19},{19,3},{4,20},{20... | collective-permute-start | bytes 1769480 | tf_op jit(solution)/shard_map/ppermute | solution.py:88
  631.8 46.5 %collective-permute-start.50 = (f32[2,96,768]{2,1,0:T(8,128)S(1)}, f32[2,96,768]{2,1,0:T(8,128)S(1)}, u32[]{:S(2)}, u32[]{:S(2)}) collective-permute-start(f32[2,96,768]{2,1,0:T(8,128)S(1)} %slice_bitcast_fusion.16), channel_id=1, source_target_pairs={{0,1},{1,0},{2,3},{3,2},{4,5},{5,4},{6,7},{7,6},{8,9},{9,8},{10,11... | collective-permute-start | bytes 1769480 | tf_op jit(solution)/shard_map/ppermute | solution.py:88
  635.9 46.7 %collective-permute-start.65 = (f32[2,96,768]{2,1,0:T(8,128)S(1)}, f32[2,96,768]{2,1,0:T(8,128)S(1)}, u32[]{:S(2)}, u32[]{:S(2)}) collective-permute-start(f32[2,96,768]{2,1,0:T(8,128)S(1)} %slice_bitcast_fusion.12), channel_id=1, source_target_pairs={{0,1},{1,0},{2,3},{3,2},{4,5},{5,4},{6,7},{7,6},{8,9},{9,8},{10,11... | collective-permute-start | bytes 1769480 | tf_op jit(solution)/shard_map/ppermute | solution.py:88
  754.2 76.5 %all-to-all-start.3 = ((f32[32,96,192]{2,1,0:T(8,128)}), f32[32,96,192]{2,1,0:T(8,128)S(1)}, u32[]{:S(2)}, u32[]{:S(2)}) async-start(f32[32,96,192]{2,1,0:T(8,128)} %bitcast.771), calls=%async_computation.3 | async-start | bytes 6291456 | tf_op jit(solution)/shard_map/all_to_all | solution.py:679
  (248 other events, 3112.3 us)

commit v2 on v1

--- a/solution.py
+++ b/solution.py
@@ -96,10 +96,8 @@
     return value
 
 
-def exchange_gather(piece, stages):
-    for stage in stages:
-        piece = jnp.stack([piece, swap(piece, stage)])
-    return piece
+def after(value, *others):
+    return lax.optimization_barrier((value, others))[0]
 
 
 def own_places():
@@ -126,120 +124,218 @@
     )
 
 
-def assemble(own_half, other_half, stages):
+def mp_walk(dims):
+    mp_dims = [bit for axis, bit in dims if axis == "mp"]
+
+    def bit_of(step, stage):
+        return (step >> (len(mp_dims) - 1 - mp_dims.index(stage[1]))) & 1
+
+    def part_of(step, places):
+        rel = sum(bit_of(step, ("mp", bit)) << bit for bit in mp_dims)
+        return rel ^ places[3]
+
+    def inner_place(step):
+        return tuple(bit_of(step, stage) if stage[0] == "mp" else 0 for stage in dims[1:]) + (0, 0)
+
+    return (bit_of, part_of, inner_place)
+
+
+def assemble(pieces, stages, edges):
     mp_count = lax.axis_size("mp")
     sizes = {axis: lax.axis_size(axis) for axis in DP}
     pairs = sizes["dh"] * sizes["dm"]
     dims = stages[::-1]
-    rows, cols = own_half.shape[-2:]
-    block = tuple(1 if axis == "mp" else 2 for axis, bit in dims) + (rows, cols)
-
-    def kernel(places, own_ref, other_ref, out_ref):
+    mp_first = dims[0][0] == "mp"
+    bit_of, part_of, inner_place = mp_walk(dims)
+    rows, cols = pieces[0].shape[-2:]
+    block = tuple(1 if axis == "mp" else 2 for axis, bit in dims[1:]) + (rows, cols)
+    widths = [last - first for first, last in zip(edges[:-1], edges[1:])]
+
+    def kernel(places, *refs):
+        piece_refs, out_refs = (refs[:4], refs[4:])
         source = pl.program_id(0)
+        step = pl.program_id(1)
         for pair in range(pairs):
             place = row_place(2 * pair, dims, places, sizes)
-
-            @pl.when(source == 0)
-            def _():
-                out_ref[0, pair, 0] = own_ref[place]
-
-            @pl.when(source == 1)
-            def _():
-                out_ref[0, pair, 0] = other_ref[place]
-
-    return pl.pallas_call(
+            later = bit_of(step, dims[0]) if mp_first else place[0]
+            for index in range(4):
+
+                @pl.when((source == index // 2) & (later == index % 2))
+                def _():
+                    value = piece_refs[index][place[1:]]
+                    for out_ref, first, last in zip(out_refs, edges[:-1], edges[1:]):
+                        out_ref[0, pair, 0] = value[:, first:last]
+
+    def in_spec(index):
+        def place(source, step, places):
+            now = jnp.where(source == index // 2, step, 0 if index // 2 else mp_count - 1)
+            if mp_first:
+                half = mp_count // 2
+                now = jnp.maximum(now, half) if index % 2 else jnp.minimum(now, half - 1)
+            return inner_place(now)
+
+        return pl.BlockSpec(block, place)
+
+    found = pl.pallas_call(
         kernel,
-        out_shape=jax.ShapeDtypeStruct((mp_count, pairs, 2, rows, cols), own_half.dtype),
+        out_shape=[
+            jax.ShapeDtypeStruct((mp_count, pairs, 2, rows, width), pieces[0].dtype)
+            for width in widths
+        ],
         grid_spec=pltpu.PrefetchScalarGridSpec(
             num_scalar_prefetch=1,
             grid=(2, mp_count),
-            in_specs=[
+            in_specs=[in_spec(index) for index in range(4)],
+            out_specs=[
                 pl.BlockSpec(
-                    block,
-                    lambda source, part, places: block_places(
-                        jnp.where(source == 0, part, mp_count - 1), dims, places
+                    (1, pairs, 1, rows, width),
+                    lambda source, step, places: (
+                        part_of(step, places),
+                        0,
+                        source ^ places[2],
+                        0,
+                        0,
                     ),
-                ),
-                pl.BlockSpec(
-                    block,
-                    lambda source, part, places: block_places(
-                        jnp.where(source == 1, part, 0), dims, places
-                    ),
-                ),
+                )
+                for width in widths
             ],
-            out_specs=pl.BlockSpec(
-                (1, pairs, 1, rows, cols),
-                lambda source, part, places: (part, 0, source ^ places[2], 0, 0),
-            ),
         ),
         cost_estimate=pl.CostEstimate(
-            flops=0, transcendentals=0, bytes_accessed=8 * own_half.size
+            flops=0, transcendentals=0, bytes_accessed=16 * pieces[0].size
         ),
         name="assemble",
-    )(own_places(), own_half, other_half)
-
-
-def weight_grads(lefts, right, edge, stages):
-    mp_count, tok_count, cols = right.shape
+    )(own_places(), *pieces)
+    return [piece.reshape(mp_count, pairs * 2 * rows, piece.shape[-1]) for piece in found]
+
+
+def pair_factors(left, right):
+    pairs = lax.axis_size("dh") * lax.axis_size("dm")
+    width, tok_count = left.shape
+    blocks = left.reshape(pairs, 2, width // (2 * pairs), tok_count)
+    mine = lax.axis_index("pr")
+    kept = lax.dynamic_index_in_dim(blocks, mine, 1, keepdims=False)
+    sent = lax.dynamic_index_in_dim(blocks, 1 - mine, 1, keepdims=False)
+    got = swap(sent, ("pr", 0))
+    flat = (width // 2, tok_count)
+    return (kept.reshape(flat), got.reshape(flat))
+
+
+def weight_grads(lefts, rights, edge, stages):
+    mp_count, tok_count, cols = rights[0].shape
     sizes = {axis: lax.axis_size(axis) for axis in DP}
     pairs = sizes["dh"] * sizes["dm"]
     dims = stages[::-1]
-    width = lefts[0].shape[0]
-    rows = width // (2 * pairs)
-    block = tuple(1 if axis == "mp" else 2 for axis, bit in dims) + (rows, cols)
-    shape = jax.ShapeDtypeStruct((2,) * len(dims) + (rows, cols), jnp.float32)
+    width = lefts[0][0].shape[0]
+    rows = width // pairs
+    mp_first = dims[0][0] == "mp"
+    bit_of, part_of, inner_place = mp_walk(dims)
+    block = tuple(1 if axis == "mp" else 2 for axis, bit in dims[1:]) + (rows, cols)
+    shape = (2,) * (len(dims) - 1) + (rows, cols)
+
+    def kept_place(step, places):
+        return inner_place(jnp.minimum(step, mp_count // 2 - 1) if mp_first else step)
+
+    def sent_place(step, places):
+        return inner_place(jnp.maximum(step, mp_count // 2) if mp_first else step)
 
     def kernel(places, *refs):
-        left_refs = refs[: len(lefts)]
-        right_ref, kept_ref, sent_ref, total_ref = refs[len(lefts) :]
-        right_part = right_ref[0]
-        total = jnp.dot(left_refs[0][...], right_part, preferred_element_type=jnp.float32)
+        left_refs = refs[: 2 * len(lefts)]
+        right_refs, (kept_ref, sent_ref) = refs[2 * len(lefts) : -2], refs[-2:]
+        step = pl.program_id(0)
+        right_parts = [right_ref[0] for right_ref in right_refs]
+        totals = [
+            jnp.dot(
+                left_refs[2 * index][...], right_parts[0], preferred_element_type=jnp.float32
+            )
+            + jnp.dot(
+                left_refs[2 * index + 1][...], right_parts[1], preferred_element_type=jnp.float32
+            )
+            for index in range(len(lefts))
+        ]
+        total = totals[0]
         if len(lefts) > 1:
-            second = jnp.dot(left_refs[1][...], right_part, preferred_element_type=jnp.float32)
             column = lax.broadcasted_iota(jnp.int32, total.shape, 1)
-            total = jnp.where(column < edge, total, second)
-        for row in range(2 * pairs):
-            total_ref[row] = total[row * rows : (row + 1) * rows]
+            total = jnp.where(column < edge, total, totals[1])
         for pair in range(pairs):
+            part = total[pair * rows : (pair + 1) * rows]
             place = row_place(2 * pair, dims, places, sizes)
-            kept_ref[place] = total_ref[2 * pair + places[2]]
-            sent_ref[place] = total_ref[2 * pair + 1 - places[2]]
-
-    spec = pl.BlockSpec(block, lambda part, places: block_places(part, dims, places))
+            first = bit_of(step, dims[0]) if mp_first else place[0]
+
+            @pl.when(first == 0)
+            def _():
+                kept_ref[place[1:]] = part
+
+            @pl.when(first == 1)
+            def _():
+                sent_ref[place[1:]] = part.astype(jnp.bfloat16)
+
+    left_spec = pl.BlockSpec((width, tok_count), lambda step, places: (0, 0))
+    right_spec = pl.BlockSpec(
+        (1, tok_count, cols), lambda step, places: (part_of(step, places), 0, 0)
+    )
     return pl.pallas_call(
         kernel,
-        out_shape=(shape, shape),
+        out_shape=(
+            jax.ShapeDtypeStruct(shape, jnp.float32),
+            jax.ShapeDtypeStruct(shape, jnp.bfloat16),
+        ),
         grid_spec=pltpu.PrefetchScalarGridSpec(
             num_scalar_prefetch=1,
             grid=(mp_count,),
-            in_specs=[
-                pl.BlockSpec((width, tok_count), lambda part, places: (0, 0)) for left in lefts
-            ]
-            + [pl.BlockSpec((1, tok_count, cols), lambda part, places: (part, 0, 0))],
-            out_specs=(spec, spec),
-            scratch_shapes=[pltpu.VMEM((2 * pairs, rows, cols), jnp.float32)],
+            in_specs=[left_spec] * (2 * len(lefts)) + [right_spec] * 2,
+            out_specs=(pl.BlockSpec(block, kept_place), pl.BlockSpec(block, sent_place)),
         ),
         cost_estimate=pl.CostEstimate(
-            flops=2 * mp_count * width * tok_count * cols,
+            flops=4 * mp_count * width * tok_count * cols,
             transcendentals=0,
-            bytes_accessed=4 * mp_count * width * cols,
+            bytes_accessed=6 * mp_count * width * cols,
         ),
         name="weight_grads",
-    )(own_places(), *lefts, right)
-
-
-def exchange_reduce(kept, sent, stages, wide):
-    total = kept + swap(sent, ("pr", 0))
-    for stage in stages[::-1]:
-        sent = total[1]
-        if not (wide and stage[0] == "mp"):
-            sent = sent.astype(jnp.bfloat16)
-        total = total[0] + swap(sent, stage).astype(jnp.float32)
-    return total
-
-
-def slow_gather(piece):
-    piece = lax.all_gather(lax.all_gather(piece, DP, axis=0, tiled=True), "mp", axis=0)
+    )(own_places(), *[left for couple in lefts for left in couple], *rights)
+
+
+class Reduction:
+    def __init__(self, kept, sent, stages, wide):
+        self.stages = stages[::-1]
+        self.wide = wide
+        self.kept = kept
+        self.sent = sent
+        self.total = None
+
+    def launch(self, sent):
+        self.sent = None
+        self.pending = swap(sent, self.stages[0])
+        self.stages = self.stages[1:]
+
+    def land(self):
+        total = self.kept + self.pending.astype(jnp.float32)
+        if self.stages:
+            sent = total[1]
+            if not (self.wide and self.stages[0][0] == "mp"):
+                sent = sent.astype(jnp.bfloat16)
+            self.kept, self.sent = (total[0], sent)
+        else:
+            self.total = total
+
+
+def advance(value, active):
+    for reduction in active:
+        if reduction.sent is None and reduction.total is None:
+            reduction.land()
+    left = [reduction for reduction in active if reduction.sent is not None]
+    value, sents = lax.optimization_barrier((value, [reduction.sent for reduction in left]))
+    for reduction, sent in zip(left, sents):
+        reduction.launch(sent)
+    return value
+
+
+def ordered_gather(piece, stages):
+    for place, stage in enumerate(stages[::-1]):
+        other_half = swap(piece, stage)
+        upper = own_bit(stage) == 1
+        piece = jnp.stack([jnp.where(upper, other_half, piece), jnp.where(upper, piece, other_half)])
+        if place > 0:
+            piece = piece.reshape((-1,) + piece.shape[2:])
     return piece
 
 
@@ -254,36 +350,36 @@
 
 def attend(queries, key_rows, values):
     scores = jnp.einsum(
-        "sqhd,skhd->shqk", queries, key_rows, preferred_element_type=jnp.float32
+        "jsqhd,jskhd->jshqk", queries, key_rows, preferred_element_type=jnp.float32
     ) * HD ** (-0.5)
     row_peak = jnp.max(scores, axis=-1, keepdims=True)
     exponent = jnp.exp(scores - row_peak)
     row_total = jnp.sum(exponent, axis=-1, keepdims=True)
     probs = (exponent / row_total).astype(jnp.bfloat16)
     attended = jnp.einsum(
-        "shqk,skhd->sqhd", probs, values, preferred_element_type=jnp.float32
+        "jshqk,jskhd->jsqhd", probs, values, preferred_element_type=jnp.float32
     ).astype(jnp.bfloat16)
     return (attended, row_peak + jnp.log(row_total))
 
 
 def attend_back(queries, key_rows, values, log_total, grad_heads):
     scores = jnp.einsum(
-        "sqhd,skhd->shqk", queries, key_rows, preferred_element_type=jnp.float32
+        "jsqhd,jskhd->jshqk", queries, key_rows, preferred_element_type=jnp.float32
     ) * HD ** (-0.5)
     probs = jnp.exp(scores - log_total)
     probs_low = probs.astype(jnp.bfloat16)
     d_values = jnp.einsum(
-        "shqk,sqhd->skhd", probs_low, grad_heads, preferred_element_type=jnp.float32
-    )
-    d_probs = jnp.einsum("sqhd,skhd->shqk", grad_heads, values, preferred_element_type=jnp.float32)
+        "jshqk,jsqhd->jskhd", probs_low, grad_heads, preferred_element_type=jnp.float32
+    )
+    d_probs = jnp.einsum("jsqhd,jskhd->jshqk", grad_heads, values, preferred_element_type=jnp.float32)
     d_scores = (probs * (d_probs - jnp.sum(d_probs * probs, axis=-1, keepdims=True))).astype(
         jnp.bfloat16
     )
     d_queries = jnp.einsum(
-        "shqk,skhd->sqhd", d_scores, key_rows, preferred_element_type=jnp.float32
+        "jshqk,jskhd->jsqhd", d_scores, key_rows, preferred_element_type=jnp.float32
     ) * HD ** (-0.5)
     d_keys = jnp.einsum(
-        "shqk,sqhd->skhd", d_scores, queries, preferred_element_type=jnp.float32
+        "jshqk,jsqhd->jskhd", d_scores, queries, preferred_element_type=jnp.float32
     ) * HD ** (-0.5)
     return (
         d_queries.astype(jnp.bfloat16),
@@ -292,119 +388,87 @@
     )
 
 
-def head_split(qkv):
-    seq_count, tok_count, parts, width = qkv.shape
+def head_split(qkv, seq_count):
+    parts, rows, width = qkv.shape
     third = width // 3
     return [
         qkv[..., slot * third : (slot + 1) * third].reshape(
-            seq_count, tok_count, parts * third // HD, HD
+            parts, seq_count, rows // seq_count, third // HD, HD
         )
         for slot in range(3)
     ]
 
 
-def layer_forward(stream, layer_weights, layer_mods):
+def tokens(value):
+    return value.reshape((value.shape[0] * value.shape[1],) + value.shape[2:])
+
+
+def product(spec, left, right):
+    return jnp.einsum(spec, left, right, preferred_element_type=jnp.float32)
+
+
+def layer_forward(stream, layer_weights, layer_mods, between):
     w_qkv, w_out, w_up, w_down = layer_weights
     shift_a, scale_a, gate_a, shift_b, scale_b, gate_b = [
         layer_mods[:, slot, None, :] for slot in range(6)
     ]
-    seq_count, tok_count = stream.shape[:2]
+    low = jnp.bfloat16
+    seq_count = stream.shape[0]
     normed_a, inv_a = layer_norm(stream)
-    in_a = (normed_a * (1.0 + scale_a) + shift_a).astype(jnp.bfloat16)
-    qkv = jnp.einsum("std,jdn->stjn", in_a, w_qkv, preferred_element_type=jnp.float32).astype(
-        jnp.bfloat16
-    )
-    heads = head_split(qkv)
+    in_a = tokens((normed_a * (1.0 + scale_a) + shift_a).astype(low))
+    qkv = product("td,jdn->jtn", in_a, w_qkv).astype(low)
+    heads = head_split(qkv, seq_count)
     attended, log_total = attend(*heads)
-    attended = attended.reshape(seq_count, tok_count, w_out.shape[0], w_out.shape[2])
-    branch_a = jnp.einsum("stjm,jdm->std", attended, w_out, preferred_element_type=jnp.float32)
-    stream_mid = stream + gate_a * branch_a
+    attended = attended.reshape(w_out.shape[0], in_a.shape[0], w_out.shape[2])
+    branch_a = product("jtm,jdm->td", attended, w_out).reshape(stream.shape)
+    stream_mid = between(stream + gate_a * branch_a)
     normed_b, inv_b = layer_norm(stream_mid)
-    in_b = (normed_b * (1.0 + scale_b) + shift_b).astype(jnp.bfloat16)
-    hidden_pre = jnp.einsum("std,jdf->stjf", in_b, w_up, preferred_element_type=jnp.float32)
-    hidden = jax.nn.gelu(hidden_pre, approximate=True).astype(jnp.bfloat16)
-    branch_b = jnp.einsum("stjf,jdf->std", hidden, w_down, preferred_element_type=jnp.float32)
-    saved_layer = (
-        normed_a,
-        inv_a,
-        in_a,
-        heads,
-        log_total,
-        attended,
-        branch_a,
-        normed_b,
-        inv_b,
-        in_b,
-        hidden_pre,
-        hidden,
-        branch_b,
-    )
-    return (stream_mid + gate_b * branch_b, saved_layer)
-
-
-def layer_backward(gradient, saved_layer, layer_weights, layer_mods):
+    in_b = tokens((normed_b * (1.0 + scale_b) + shift_b).astype(low))
+    hidden_pre = product("td,jdf->jtf", in_b, w_up)
+    hidden = jax.nn.gelu(hidden_pre, approximate=True).astype(low)
+    branch_b = product("jtf,jdf->td", hidden, w_down).reshape(stream.shape)
+    saved_a = (normed_a, inv_a, in_a, heads, log_total, attended, branch_a)
+    saved_b = (normed_b, inv_b, in_b, hidden_pre, hidden, branch_b)
+    return (stream_mid + gate_b * branch_b, saved_a, saved_b)
+
+
+def mlp_backward(gradient, saved_b, layer_weights, layer_mods):
     w_qkv, w_out, w_up, w_down = layer_weights
-    (
-        normed_a,
-        inv_a,
-        in_a,
-        heads,
-        log_total,
-        attended,
-        branch_a,
-        normed_b,
-        inv_b,
-        in_b,
-        hidden_pre,
-        hidden,
-        branch_b,
-    ) = saved_layer
-    shift_a, scale_a, gate_a, shift_b, scale_b, gate_b = [
-        layer_mods[:, slot, None, :] for slot in range(6)
-    ]
-    seq_count, tok_count = gradient.shape[:2]
+    normed_b, inv_b, in_b, hidden_pre, hidden, branch_b = saved_b
+    scale_b, gate_b = [layer_mods[:, slot, None, :] for slot in (4, 5)]
     low = jnp.bfloat16
-    d_branch_b = (gate_b * gradient).astype(low)
+    d_branch_b = tokens((gate_b * gradient).astype(low))
     d_gate_b = jnp.sum(gradient * branch_b, axis=1)
-    d_hidden = jnp.einsum("std,jdf->stjf", d_branch_b, w_down, preferred_element_type=jnp.float32)
+    d_hidden = product("td,jdf->jtf", d_branch_b, w_down)
     d_pre = jax.vjp(lambda value_in: jax.nn.gelu(value_in, approximate=True), hidden_pre)[1](
         d_hidden
     )[0].astype(low)
-    d_in_b = jnp.einsum("stjf,jdf->std", d_pre, w_up, preferred_element_type=jnp.float32)
+    d_in_b = product("jtf,jdf->td", d_pre, w_up).reshape(gradient.shape)
     d_scale_b = jnp.sum(d_in_b * normed_b, axis=1)
     d_shift_b = jnp.sum(d_in_b, axis=1)
     d_mid = gradient + norm_back(normed_b, inv_b, d_in_b * (1.0 + scale_b))
-    d_branch_a = (gate_a * d_mid).astype(low)
+    factors = (((in_b.T,), d_pre), ((d_branch_b.T,), hidden))
+    return (d_mid, [d_shift_b, d_scale_b, d_gate_b], factors)
+
+
+def attention_backward(d_mid, saved_a, layer_weights, layer_mods):
+    w_qkv, w_out, w_up, w_down = layer_weights
+    normed_a, inv_a, in_a, heads, log_total, attended, branch_a = saved_a
+    scale_a, gate_a = [layer_mods[:, slot, None, :] for slot in (1, 2)]
+    low = jnp.bfloat16
+    d_branch_a = tokens((gate_a * d_mid).astype(low))
     d_gate_a = jnp.sum(d_mid * branch_a, axis=1)
-    d_attended = jnp.einsum(
-        "std,jdm->stjm", d_branch_a, w_out, preferred_element_type=jnp.float32
-    ).astype(low)
-    parts = w_out.shape[0]
+    d_attended = product("td,jdm->jtm", d_branch_a, w_out).astype(low)
     d_heads = attend_back(*heads, log_total, d_attended.reshape(heads[0].shape))
     d_qkv = jnp.concatenate(
-        [piece.reshape(seq_count, tok_count, parts, -1) for piece in d_heads], axis=-1
-    )
-    d_in_a = jnp.einsum("stjn,jdn->std", d_qkv, w_qkv, preferred_element_type=jnp.float32)
+        [piece.reshape(attended.shape[:2] + (-1,)) for piece in d_heads], axis=-1
+    )
+    d_in_a = product("jtn,jdn->td", d_qkv, w_qkv).reshape(d_mid.shape)
     d_scale_a = jnp.sum(d_in_a * normed_a, axis=1)
     d_shift_a = jnp.sum(d_in_a, axis=1)
     grad_in = d_mid + norm_back(normed_a, inv_a, d_in_a * (1.0 + scale_a))
-    d_mods = jnp.stack([d_shift_a, d_scale_a, d_gate_a, d_shift_b, d_scale_b, d_gate_b], axis=1)
-
-    def flat(value):
-        return value.reshape((seq_count * tok_count,) + value.shape[2:])
-
-    def parted(value):
-        return flat(value).transpose(1, 0, 2)
-
-    factors = (
-        ((flat(in_b).T,), parted(d_pre)),
-        ((flat(d_branch_b).T,), parted(hidden)),
-        (
-            (flat(in_a).T, flat(d_branch_a).T),
-            parted(jnp.concatenate([d_qkv, attended], axis=-1)),
-        ),
-    )
-    return (grad_in, d_mods, factors)
+    factors = (((in_a.T, d_branch_a.T), jnp.concatenate([d_qkv, attended], axis=-1)),)
+    return (grad_in, [d_shift_a, d_scale_a, d_gate_a], factors)
 
 
 def polar_factor(gram):
@@ -474,26 +538,11 @@
     fast = row_count % 16 == 0
     y_stages, x_stages = (axis_bits("dh"), axis_bits("dm")[::-1])
     routes = [
-        [
-            mp_stages + y_stages + x_stages,
-            first + mp_stages + last,
-            mp_stages + x_stages + y_stages,
-        ]
-        for first, last in ((x_stages, y_stages), (y_stages, x_stages))
+        y_stages + mp_stages + x_stages,
+        x_stages + y_stages + mp_stages,
+        mp_stages + x_stages + y_stages,
     ]
-    assert LAYERS == len(routes)
-
-    def gather_whole(piece, stages):
-        if not fast:
-            return slow_gather(piece)
-        piece = exchange_gather(piece, stages)
-        return assemble(piece, swap(piece, ("pr", 0)), stages)
-
-    def reduce_whole(lefts, right, stages, wide):
-        if not fast:
-            return slow_reduce(lefts, right, width_qkv)
-        kept, sent = weight_grads(lefts, right, width_qkv, stages)
-        return exchange_reduce(kept, sent, stages, wide)
+    edges = [(0, up_proj.shape[2]), (0, up_proj.shape[2]), (0, width_qkv, width_qkv + width_out)]
 
     def oriented(qkv, out, up, down):
         layers = []
@@ -518,17 +567,55 @@
         out = jnp.stack([pieces[2][:, width_qkv:].T for pieces in layers])
         return (qkv, out, up, down)
 
-    gathered = []
-    for pieces in oriented(
+    def reduce_whole(lefts, right, stages, wide):
+        couples = [pair_factors(left, right) for left in lefts]
+        rights = (right, swap(right, ("pr", 0)))
+        kept, sent = weight_grads(couples, rights, width_qkv, stages)
+        return Reduction(kept, sent, stages, wide)
+
+    shards = oriented(
         qkv_proj.astype(low), out_proj.astype(low), up_proj.astype(low), down_proj.astype(low)
-    ):
-        up_all, down_all, rest_all = [
-            gather_whole(piece, stages).reshape(mp_count, dp_count * row_count, piece.shape[1])
-            for piece, stages in zip(pieces, routes[len(gathered)])
+    )
+    pieces = [list(shard) for shard in shards]
+    depths = [0] * LAYERS
+    last_depth = len(routes[0]) - 1
+
+    def gather_round(*layers):
+        ready = lax.optimization_barrier([pieces[layer_index] for layer_index in layers])
+        for layer_index, now in zip(layers, ready):
+            depth = depths[layer_index]
+            got = [swap(piece, stages[depth]) for piece, stages in zip(now, routes)]
+            if depth < last_depth:
+                pieces[layer_index] = [jnp.stack(both) for both in zip(now, got)]
+            else:
+                pieces[layer_index] = [
+                    (own, other, swap(own, ("pr", 0)), swap(other, ("pr", 0)))
+                    for own, other in zip(now, got)
+                ]
+            depths[layer_index] = depth + 1
+
+    def whole(piece):
+        piece = lax.all_gather(piece, ("mp",) + DP, axis=0, tiled=True)
+        return piece.reshape(mp_count, dp_count * row_count, piece.shape[1])
+
+    def layer_weights_of(layer_index):
+        if not fast:
+            up, down, rest = [whole(piece) for piece in pieces[layer_index]]
+            return (rest[..., :width_qkv], rest[..., width_qkv:], up, down)
+        found = [
+            assemble(pieces[layer_index][slot], routes[slot], edges[slot]) for slot in (2, 0, 1)
         ]
-        gathered.append(
-            (rest_all[..., :width_qkv], rest_all[..., width_qkv:], up_all, down_all)
-        )
+        return found[0] + found[1] + found[2]
+
+    def gather_dp(piece):
+        if not fast:
+            piece = lax.all_gather(piece, DP, axis=0)
+        else:
+            piece = ordered_gather(piece, dp_stages)
+        return piece.transpose(1, 0, 2).reshape(piece.shape[1], -1)
+
+    if fast:
+        gather_round(0)
 
     tables_low = tables.astype(low)
     time_low = time_proj.astype(low)
@@ -536,9 +623,9 @@
     time_in = tables_low[PATCH_IN : PATCH_IN + FREQ]
     class_table = tables_low[PATCH_IN + FREQ : PATCH_IN + FREQ + CLASSES]
     ends = jnp.concatenate([tables_low[:PATCH_IN], tables_low[PATCH_IN + FREQ + CLASSES :]], axis=0)
-    index_rows = lax.all_gather(jnp.stack([labels, time_index]), DP, axis=1, tiled=True)
+    index_rows = gather_dp(jnp.stack([labels, time_index]))
     every_label, every_time = (index_rows[0], index_rows[1])
-    ends_all = lax.all_gather(ends, DP, axis=1, tiled=True)
+    ends_all = gather_dp(ends)
     patch_w, head_t = (ends_all[:PATCH_IN], ends_all[PATCH_IN:])
     every_count = every_time.shape[0]
     freq = freq_table(every_time).astype(low)
@@ -578,9 +665,26 @@
         for layer_index in range(LAYERS)
     ]
     saved_all = []
+    weights_all = []
+    if fast:
+        gather_round(0)
+        gather_round(0, 1)
+        gather_round(0, 1)
+        pieces[1] = after(pieces[1], [halves[1] for halves in pieces[0]])
+        gather_round(1)
+
+    def between(value):
+        if fast and layer_index == 0:
+            value, pieces[1] = lax.optimization_barrier((value, pieces[1]))
+            gather_round(1)
+        return value
+
     for layer_index in range(LAYERS):
-        stream, saved_layer = layer_forward(stream, gathered[layer_index], layer_mods[layer_index])
-        saved_all.append(saved_layer)
+        weights_all.append(layer_weights_of(layer_index))
+        stream, saved_a, saved_b = layer_forward(
+            stream, weights_all[layer_index], layer_mods[layer_index], between
+        )
+        saved_all.append((saved_a, saved_b))
     base = 6 * LAYERS * D
     shift_f = mod_rows[:, None, base : base + D]
     scale_f = mod_rows[:, None, base + D : base + 2 * D]
@@ -598,15 +702,43 @@
     gradient = norm_back(normed_f, inv_f, d_in_f * (1.0 + scale_f))
     mod_grads = [None] * LAYERS
     layer_grads = [None] * LAYERS
+    active = []
+
+    def collect(factors, stages_of):
+        found = []
+        for (lefts, right), stages in zip(factors, stages_of):
+            if fast:
+                found.append(reduce_whole(lefts, right, stages, len(lefts) > 1))
+            else:
+                found.append(slow_reduce(lefts, right, width_qkv))
+        return found
+
     for layer_index in reversed(range(LAYERS)):
-        gradient, d_mods, factors = layer_backward(
-            gradient, saved_all[layer_index], gathered[layer_index], layer_mods[layer_index]
+        saved_a, saved_b = saved_all[layer_index]
+        weights = weights_all[layer_index]
+        d_mid, d_mods_b, factors = mlp_backward(
+            gradient, saved_b, weights, layer_mods[layer_index]
         )
-        mod_grads[layer_index] = d_mods.reshape(seq_count, 6 * D)
-        layer_grads[layer_index] = [
-            reduce_whole(lefts, right, stages, len(lefts) > 1)
-            for (lefts, right), stages in zip(factors, routes[layer_index])
-        ]
+        found = collect(factors, routes[:2])
+        active += found
+        if fast:
+            d_mid = advance(d_mid, active)
+        gradient, d_mods_a, factors = attention_backward(
+            d_mid, saved_a, weights, layer_mods[layer_index]
+        )
+        last = collect(factors, routes[2:])
+        active += last
+        if fast:
+            gradient = advance(gradient, active)
+        mod_grads[layer_index] = jnp.concatenate(d_mods_a + d_mods_b, axis=1)
+        layer_grads[layer_index] = found + last
+    if fast:
+        mod_grads, (d_shift_f, d_scale_f, d_head) = after(
+            (mod_grads, (d_shift_f, d_scale_f, d_head)), gradient
+        )
+        while any(reduction.total is None for reduction in active):
+            advance((), active)
+        layer_grads = [[reduction.total for reduction in found] for found in layer_grads]
     d_first = gradient.astype(low)
     d_patch = jnp.einsum("stp,std->pd", noisy, d_first, preferred_element_type=jnp.float32)
     d_ends = exchange_sum(jnp.concatenate([d_patch, d_head], axis=0), order[::-1])
@@ -623,7 +755,7 @@
     )
     d_condition = jax.vjp(jax.nn.silu, condition)[1](d_cond_act)[0].astype(low)
     d_class = jnp.einsum("sc,sd->cd", onehot, d_condition, preferred_element_type=jnp.float32)
-    d_condition_all = lax.all_gather(d_condition, DP, axis=1, tiled=True)
+    d_condition_all = gather_dp(d_condition)
     grad_time = jnp.einsum("se,sd->ed", time_act, d_condition_all, preferred_element_type=jnp.float32)
     d_time_act = jnp.einsum(
         "sd,ed->se", d_condition_all, time_low, preferred_element_type=jnp.float32

time: 1020 us -> 1010 us (level)
  other arithmetic: 150 us -> 111 us
  local copies, waits for them, and re-layouts: 119 us -> 151 us
  blocking collectives: 28.4 us -> 0 us
  waiting for transfers between devices: 354 us -> 378 us
    all_gather x3 -> x0, blocking collectives: 28.4 us -> none  [the longest x1 10.4 us: body(): lax.all_gather(jnp.stack([labels, time_index]), DP, axis=1, tiled=True)]
    another operation x27 -> x39, other arithmetic: 37.7 us -> 20.7 us  [the longest x18 20.1 us: gather_round(): pieces[layer_index] = [jnp.stack(both) for both in zip(now, got)]]
    transpose x6 -> x2, other arithmetic: 16.8 us -> 2.74 us  [the longest x1 1.42 us: attention_backward(): factors = (((in_a.T, d_branch_a.T), jnp.concatenate([d_qkv, attended], ax...]
    squeeze x4 -> x13, local copies, waits for them, and re-layouts: 1.55 us -> 14.9 us  [the longest x8 13.1 us: pair_factors(): sent = lax.dynamic_index_in_dim(blocks, 1 - mine, 1, keepdims=False)]
    add x24 -> x20, other arithmetic: 30.2 us -> 17.6 us  [the longest x18 15.5 us: land(): total = self.kept + self.pending.astype(jnp.float32)]
    transpose x0 -> x9, local copies, waits for them, and re-layouts: none -> 12.3 us  [the longest x4 6.66 us: mlp_backward(): factors = (((in_b.T,), d_pre), ((d_branch_b.T,), hidden))]
    ppermute x75 -> x98, waiting for transfers between devices: 256 us -> 268 us  [swap(): lax.ppermute(value, axis, [(place, place ^ 1 << bit) for place in range(l...]
    all_to_all x1, waiting for transfers between devices: 0.01 us -> 10.9 us  [body(): lax.all_to_all(d_mod_sent, ALL, split_axis=0, concat_axis=0, tiled=True)]
  transfers between devices with their start and end apart: 80 -> 103, of which waited for: 36 -> 41; matrix products, arithmetic and copies ran while one was open for 20% -> 26% of each run, Pallas kernels for 8% -> 8%
where the time goes in v2:
time: 1010 us; the launch traced here: 1000 us
  waiting for transfers between devices  378 us (37%)
  matrix products  158 us (16%)
  local copies, waits for them, and re-layouts  151 us (15%)
  other arithmetic  111 us (11%)
  starting transfers between devices  98.8 us (10%)
  Pallas kernels  92.6 us (9%)
  between operations  14.5 us (1%)
    ppermute x98, waiting for transfers between devices, swap(): lax.ppermute(value, axis, [(place, place ^ 1 << bit) for place in range(l...  268 us
    ppermute x98, starting transfers between devices, swap(): lax.ppermute(value, axis, [(place, place ^ 1 << bit) for place in range(l...  82 us
    all_to_all x1, waiting for transfers between devices, body(): got = lax.all_to_all(sent, MATS, split_axis=0, concat_axis=0, tiled=True)  72.4 us
    dot_general x19, matrix products, mat_dot(): return jnp.dot(left, right, precision=lax.Precision.HIGH)  65 us
    dot_general x16, matrix products, product(): return jnp.einsum(spec, left, right, preferred_element_type=jnp.float32)  63.6 us
    pallas_call x6, Pallas kernels, assemble(): pl.pallas_call(kernel, out_shape=[jax.ShapeDtypeStruct((mp_count, pairs,...  52.3 us
    unnamed x458, local copies, waits for them, and re-layouts  45.3 us
    pallas_call x6, Pallas kernels, weight_grads(): pl.pallas_call(kernel, out_shape=(jax.ShapeDtypeStruct(shape, jnp.float32...  40.3 us
  transfers between devices with their start and end apart: 103, of which 41 were waited for; matrix products, arithmetic and copies ran while one was open for 26% of the time, Pallas kernels for 8%

profile of v2, /device:TPU:0, one launch (start us, length us, event | category | flops | bytes accessed | tf_op | source)
XLA Modules:
  0.0 1003.4 jit_solution(9451774554788094889)
XLA Ops:
  39.7 8.0 collective-permute-done.10
  62.0 14.2 %collective-permute-done.17 = bf16[96,768]{1,0:T(8,128)(2,1)S(1)} collective-permute-done((bf16[96,768]{1,0:T(8,128)(2,1)S(1)}, bf16[96,768]{1,0:T(8,128)(2,1)S(1)}, u32[]{:S(2)}, u32[]{:S(2)}) %collective-permute-start.17) | collective-permute-done | bytes 147488 | tf_op jit(solution)/shard_map/ppermute | solution.py:88
  91.3 10.1 %collective-permute-done.12 = bf16[2,2,96,768]{3,2,1,0:T(8,128)(2,1)S(1)} collective-permute-done((bf16[2,2,96,768]{3,2,1,0:T(8,128)(2,1)S(1)}, bf16[2,2,96,768]{3,2,1,0:T(8,128)(2,1)S(1)}, u32[]{:S(2)}, u32[]{:S(2)}) %collective-permute-start.12) | collective-permute-done | bytes 589856 | tf_op jit(solution)/shard_map/ppermute | solution.py:88
  117.0 19.6 %collective-permute-done.21 = bf16[2,96,768]{2,1,0:T(8,128)(2,1)} collective-permute-done((bf16[2,96,768]{2,1,0:T(8,128)(2,1)}, bf16[2,96,768]{2,1,0:T(8,128)(2,1)}, u32[]{:S(2)}, u32[]{:S(2)}) %collective-permute-start.21) | collective-permute-done | bytes 294944 | tf_op jit(solution)/shard_map/ppermute | solution.py:88
  157.9 8.7 collective-permute-done.28
  169.0 12.6 %collective-permute-done.27 = bf16[2,2,96,768]{3,2,1,0:T(8,128)(2,1)} collective-permute-done((bf16[2,2,96,768]{3,2,1,0:T(8,128)(2,1)}, bf16[2,2,96,768]{3,2,1,0:T(8,128)(2,1)}, u32[]{:S(2)}, u32[]{:S(2)}) %collective-permute-start.27) | collective-permute-done | bytes 589856 | tf_op jit(solution)/shard_map/ppermute | solution.py:88
  185.6 9.1 assemble.6
  208.1 8.6 assemble.8
  218.6 8.4 assemble.7
  245.9 9.1 assemble.9
  265.0 8.1 assemble.10
  281.1 9.0 assemble.11
  377.5 12.7 %collective-permute-done.47 = bf16[2,2,2,96,768]{4,3,2,1,0:T(8,128)(2,1)} collective-permute-done((bf16[2,2,2,96,768]{4,3,2,1,0:T(8,128)(2,1)}, bf16[2,2,2,96,768]{4,3,2,1,0:T(8,128)(2,1)}, u32[]{:S(2)}, u32[]{:S(2)}) %collective-permute-start.47) | collective-permute-done | bytes 1179680 | tf_op jit(solution)/shard_map/ppermute | solution.py:88
  451.8 9.2 collective-permute-done.53
  508.3 20.7 %collective-permute-done.58 = bf16[2,96,768]{2,1,0:T(8,128)(2,1)S(1)} collective-permute-done((bf16[2,96,768]{2,1,0:T(8,128)(2,1)S(1)}, bf16[2,96,768]{2,1,0:T(8,128)(2,1)S(1)}, u32[]{:S(2)}, u32[]{:S(2)}) %collective-permute-start.58) | collective-permute-done | bytes 294944 | tf_op jit(solution)/shard_map/ppermute | solution.py:88
  533.8 24.5 %collective-permute-done.61 = bf16[2,2,2,96,768]{4,3,2,1,0:T(8,128)(2,1)S(1)} collective-permute-done((bf16[2,2,2,96,768]{4,3,2,1,0:T(8,128)(2,1)S(1)}, bf16[2,2,2,96,768]{4,3,2,1,0:T(8,128)(2,1)S(1)}, u32[]{:S(2)}, u32[]{:S(2)}) %collective-permute-start.61) | collective-permute-done | bytes 1179680 | tf_op jit(solution)/shard_map/ppermute | solution.py:88
  593.6 10.9 %all-to-all-done.2 = bf16[32,2,1344]{2,1,0:T(2,128)(2,1)} async-done(((bf16[32,2,1344]{2,1,0:T(2,128)(2,1)}), bf16[32,2,1344]{2,1,0:T(2,128)(2,1)}, u32[]{:S(2)}, u32[]{:S(2)}) %all-to-all-start.2) | async-done | bytes 172064 | tf_op jit(solution)/shard_map/all_to_all | solution.py:751
  638.2 8.4 collective-permute-done.76
  659.7 10.3 %collective-permute-done.80 = bf16[2,96,768]{2,1,0:T(8,128)(2,1)S(1)} collective-permute-done((bf16[2,96,768]{2,1,0:T(8,128)(2,1)}, bf16[2,96,768]{2,1,0:T(8,128)(2,1)S(1)}, u32[]{:S(2)}, u32[]{:S(2)}) %collective-permute-start.80) | collective-permute-done | bytes 294944 | tf_op jit(solution)/shard_map/ppermute | solution.py:88
  683.4 7.9 collective-permute-done.85
  692.9 9.2 collective-permute-done.89
  757.3 72.4 %all-to-all-done.3 = f32[32,96,192]{2,1,0:T(8,128)S(1)} async-done(((f32[32,96,192]{2,1,0:T(8,128)}), f32[32,96,192]{2,1,0:T(8,128)S(1)}, u32[]{:S(2)}, u32[]{:S(2)}) %all-to-all-start.3) | async-done | bytes 2359328 | tf_op jit(solution)/shard_map/all_to_all | solution.py:811
  848.2 26.8 %collective-permute-done.96 = f32[384,768]{1,0:T(8,128)S(1)} collective-permute-done((f32[384,768]{1,0:T(8,128)S(1)}, f32[384,768]{1,0:T(8,128)S(1)}, u32[]{:S(2)}, u32[]{:S(2)}) %collective-permute-start.96) | collective-permute-done | bytes 1179680 | tf_op jit(solution)/shard_map/ppermute | solution.py:88
  963.9 26.3 %all-to-all-done.4 = bf16[32,96,192]{2,1,0:T(8,128)(2,1)S(1)} async-done(((bf16[32,96,192]{2,1,0:T(8,128)(2,1)}), bf16[32,96,192]{2,1,0:T(8,128)(2,1)S(1)}, u32[]{:S(2)}, u32[]{:S(2)}) %all-to-all-start.4) | async-done | bytes 1179680 | tf_op jit(solution)/shard_map/all_to_all | solution.py:819
  (1012 shorter events, 624.0 us)
Async XLA Ops:
  32.6 73.1 %all-to-all-start = ((f32[8,32,96]{2,1,0:T(8,128)}), f32[8,32,96]{2,1,0:T(8,128)}, u32[]{:S(2)}, u32[]{:S(2)}) async-start(f32[8,32,96]{2,1,0:T(8,128)} %bitcast.867), calls=%async_computation | async-start | bytes 262144 | tf_op jit(solution)/shard_map/all_to_all | solution.py:637
  103.7 48.2 %collective-permute-start.25 = (bf16[2,2,2,96,768]{4,3,2,1,0:T(8,128)(2,1)}, bf16[2,2,2,96,768]{4,3,2,1,0:T(8,128)(2,1)}, u32[]{:S(2)}, u32[]{:S(2)}) collective-permute-start(bf16[2,2,2,96,768]{4,3,2,1,0:T(8,128)(2,1)} %pad_maximum_fusion.4.refs_0_), channel_id=1, source_target_pairs={{0,1},{1,0},{2,3},{3,2},{4,5},{5,4},{6,7},{7,6},{8,9},{9,8},{10,11... | collective-permute-start | bytes 3538952 | tf_op jit(solution)/shard_map/ppermute | solution.py:88
  103.7 40.3 %collective-permute-start.18 = (bf16[2,2,2,96,768]{4,3,2,1,0:T(8,128)(2,1)S(1)}, bf16[2,2,2,96,768]{4,3,2,1,0:T(8,128)(2,1)}, u32[]{:S(2)}, u32[]{:S(2)}) collective-permute-start(bf16[2,2,2,96,768]{4,3,2,1,0:T(8,128)(2,1)S(1)} %pad_maximum_fusion.5.refs_0_), channel_id=1, source_target_pairs={{0,16},{16,0},{1,17},{17,1},{2,18},{18,2},{3,19},{19,3},{4,20},{20... | collective-permute-start | bytes 3538952 | tf_op jit(solution)/shard_map/ppermute | solution.py:88
  104.2 47.7 %collective-permute-start.24 = (bf16[2,2,2,96,768]{4,3,2,1,0:T(8,128)(2,1)}, bf16[2,2,2,96,768]{4,3,2,1,0:T(8,128)(2,1)}, u32[]{:S(2)}, u32[]{:S(2)}) collective-permute-start(bf16[2,2,2,96,768]{4,3,2,1,0:T(8,128)(2,1)} %pad_maximum_fusion.3.refs_0_), channel_id=1, source_target_pairs={{0,8},{8,0},{1,9},{9,1},{2,10},{10,2},{3,11},{11,3},{4,12},{12,4},... | collective-permute-start | bytes 3538952 | tf_op jit(solution)/shard_map/ppermute | solution.py:88
  114.0 38.5 %all-to-all-start.1 = ((f32[32,1,2688]{2,1,0:T(1,128)}), f32[32,1,2688]{2,1,0:T(1,128)S(1)}, u32[]{:S(2)}, u32[]{:S(2)}) async-start(f32[32,1,2688]{2,1,0:T(1,128)} %copy.365), calls=%async_computation.1 | async-start | bytes 688128 | tf_op jit(solution)/shard_map/all_to_all | solution.py:645
  142.0 43.6 %collective-permute-start.19 = (bf16[2,2,2,96,768]{4,3,2,1,0:T(8,128)(2,1)S(1)}, bf16[2,2,2,96,768]{4,3,2,1,0:T(8,128)(2,1)}, u32[]{:S(2)}, u32[]{:S(2)}) collective-permute-start(bf16[2,2,2,96,768]{4,3,2,1,0:T(8,128)(2,1)S(1)} %pad_maximum_fusion.5.refs_0_), channel_id=1, source_target_pairs={{0,4},{4,0},{1,5},{5,1},{2,6},{6,2},{3,7},{7,3},{8,12},{12,8},{9,1... | collective-permute-start | bytes 3538952 | tf_op jit(solution)/shard_map/ppermute | solution.py:88
  144.0 41.6 %collective-permute-start.20 = (bf16[2,2,2,96,768]{4,3,2,1,0:T(8,128)(2,1)}, bf16[2,2,2,96,768]{4,3,2,1,0:T(8,128)(2,1)}, u32[]{:S(2)}, u32[]{:S(2)}) collective-permute-start(bf16[2,2,2,96,768]{4,3,2,1,0:T(8,128)(2,1)} %collective-permute-done.18.refs_1_), channel_id=1, source_target_pairs={{0,4},{4,0},{1,5},{5,1},{2,6},{6,2},{3,7},{7,3},{8,12},{12,8},{9,1... | collective-permute-start | bytes 3538952 | tf_op jit(solution)/shard_map/ppermute | solution.py:88
  166.6 41.3 %collective-permute-start.31 = (bf16[2,2,2,96,768]{4,3,2,1,0:T(8,128)(2,1)}, bf16[2,2,2,96,768]{4,3,2,1,0:T(8,128)(2,1)}, u32[]{:S(2)}, u32[]{:S(2)}) collective-permute-start(bf16[2,2,2,96,768]{4,3,2,1,0:T(8,128)(2,1)} %pad_maximum_fusion.4.refs_0_), channel_id=1, source_target_pairs={{0,4},{4,0},{1,5},{5,1},{2,6},{6,2},{3,7},{7,3},{8,12},{12,8},{9,1... | collective-permute-start | bytes 3538952 | tf_op jit(solution)/shard_map/ppermute | solution.py:88
  216.7 64.4 %collective-permute-start.40 = (bf16[2,2,2,96,768]{4,3,2,1,0:T(8,128)(2,1)}, bf16[2,2,2,96,768]{4,3,2,1,0:T(8,128)(2,1)}, u32[]{:S(2)}, u32[]{:S(2)}) collective-permute-start(bf16[2,2,2,96,768]{4,3,2,1,0:T(8,128)(2,1)} %pad_maximum_fusion.7.refs_0_), channel_id=1, source_target_pairs={{0,4},{4,0},{1,5},{5,1},{2,6},{6,2},{3,7},{7,3},{8,12},{12,8},{9,1... | collective-permute-start | bytes 3538952 | tf_op jit(solution)/shard_map/ppermute | solution.py:88
  241.8 190.6 %collective-permute-start.57 = (bf16[4,256,768]{2,1,0:T(8,128)(2,1)}, bf16[4,256,768]{2,1,0:T(8,128)(2,1)}, u32[]{:S(2)}, u32[]{:S(2)}) collective-permute-start(bf16[4,256,768]{2,1,0:T(8,128)(2,1)} %get-tuple-element.437.refs_2_), channel_id=1, source_target_pairs={{0,4},{4,0},{1,5},{5,1},{2,6},{6,2},{3,7},{7,3},{8,12},{12,8},{9,1... | collective-permute-start | bytes 4718600 | tf_op jit(solution)/shard_map/ppermute | solution.py:88
  245.4 35.7 %collective-permute-start.41 = (bf16[2,2,2,96,768]{4,3,2,1,0:T(8,128)(2,1)}, bf16[2,2,2,96,768]{4,3,2,1,0:T(8,128)(2,1)}, u32[]{:S(2)}, u32[]{:S(2)}) collective-permute-start(bf16[2,2,2,96,768]{4,3,2,1,0:T(8,128)(2,1)} %collective-permute-done.39.refs_1_), channel_id=1, source_target_pairs={{0,4},{4,0},{1,5},{5,1},{2,6},{6,2},{3,7},{7,3},{8,12},{12,8},{9,1... | collective-permute-start | bytes 3538952 | tf_op jit(solution)/shard_map/ppermute | solution.py:88
  281.0 44.9 %collective-permute-start.45 = (bf16[4,256,768]{2,1,0:T(8,128)(2,1)}, bf16[4,256,768]{2,1,0:T(8,128)(2,1)}, u32[]{:S(2)}, u32[]{:S(2)}) collective-permute-start(bf16[4,256,768]{2,1,0:T(8,128)(2,1)} %get-tuple-element.443.refs_2_), channel_id=1, source_target_pairs={{0,4},{4,0},{1,5},{5,1},{2,6},{6,2},{3,7},{7,3},{8,12},{12,8},{9,1... | collective-permute-start | bytes 4718600 | tf_op jit(solution)/shard_map/ppermute | solution.py:88
  360.2 41.0 %collective-permute-start.50 = (bf16[4,256,768]{2,1,0:T(8,128)(2,1)}, bf16[4,256,768]{2,1,0:T(8,128)(2,1)}, u32[]{:S(2)}, u32[]{:S(2)}) collective-permute-start(bf16[4,256,768]{2,1,0:T(8,128)(2,1)} %pad_maximum_fusion.1.refs_4_), channel_id=1, source_target_pairs={{0,4},{4,0},{1,5},{5,1},{2,6},{6,2},{3,7},{7,3},{8,12},{12,8},{9,1... | collective-permute-start | bytes 4718600 | tf_op jit(solution)/shard_map/ppermute | solution.py:88
  429.2 35.8 %collective-permute-start.55 = (bf16[4,256,768]{2,1,0:T(8,128)(2,1)}, bf16[4,256,768]{2,1,0:T(8,128)(2,1)}, u32[]{:S(2)}, u32[]{:S(2)}) collective-permute-start(bf16[4,256,768]{2,1,0:T(8,128)(2,1)} %copy-done.206), channel_id=1, source_target_pairs={{0,4},{4,0},{1,5},{5,1},{2,6},{6,2},{3,7},{7,3},{8,12},{12,8},{9,1... | collective-permute-start | bytes 4718600 | tf_op jit(solution)/shard_map/ppermute | solution.py:88
  488.0 72.9 %collective-permute-start.65 = (bf16[4,256,768]{2,1,0:T(8,128)(2,1)}, bf16[4,256,768]{2,1,0:T(8,128)(2,1)}, u32[]{:S(2)}, u32[]{:S(2)}) collective-permute-start(bf16[4,256,768]{2,1,0:T(8,128)(2,1)} %pad_maximum_fusion.2.refs_4_), channel_id=1, source_target_pairs={{0,4},{4,0},{1,5},{5,1},{2,6},{6,2},{3,7},{7,3},{8,12},{12,8},{9,1... | collective-permute-start | bytes 4718600 | tf_op jit(solution)/shard_map/ppermute | solution.py:88
  488.9 71.9 %collective-permute-start.64 = (bf16[4,96,256]{2,1,0:T(8,128)(2,1)}, bf16[4,96,256]{2,1,0:T(8,128)(2,1)}, u32[]{:S(2)}, u32[]{:S(2)}) collective-permute-start(bf16[4,96,256]{2,1,0:T(8,128)(2,1)} %get-tuple-element.373), channel_id=1, source_target_pairs={{0,4},{4,0},{1,5},{5,1},{2,6},{6,2},{3,7},{7,3},{8,12},{12,8},{9,1... | collective-permute-start | bytes 589832 | tf_op jit(solution)/shard_map/ppermute | solution.py:88
  495.0 37.4 %collective-permute-start.62 = (bf16[2,2,2,96,768]{4,3,2,1,0:T(8,128)(2,1)}, bf16[2,2,2,96,768]{4,3,2,1,0:T(8,128)(2,1)S(1)}, u32[]{:S(2)}, u32[]{:S(2)}) collective-permute-start(bf16[2,2,2,96,768]{4,3,2,1,0:T(8,128)(2,1)} %get-tuple-element.155), channel_id=1, source_target_pairs={{0,1},{1,0},{2,3},{3,2},{4,5},{5,4},{6,7},{7,6},{8,9},{9,8},{10,11... | collective-permute-start | bytes 3538952 | tf_op jit(solution)/shard_map/ppermute | solution.py:88
  568.7 78.8 %collective-permute-start.79 = (bf16[2,2,2,96,768]{4,3,2,1,0:T(8,128)(2,1)}, bf16[2,2,2,96,768]{4,3,2,1,0:T(8,128)(2,1)}, u32[]{:S(2)}, u32[]{:S(2)}) collective-permute-start(bf16[2,2,2,96,768]{4,3,2,1,0:T(8,128)(2,1)} %get-tuple-element.167), channel_id=1, source_target_pairs={{0,16},{16,0},{1,17},{17,1},{2,18},{18,2},{3,19},{19,3},{4,20},{20... | collective-permute-start | bytes 3538952 | tf_op jit(solution)/shard_map/ppermute | solution.py:88
  570.2 65.8 %collective-permute-start.78 = (bf16[2,2,96,768]{3,2,1,0:T(8,128)(2,1)}, bf16[2,2,96,768]{3,2,1,0:T(8,128)(2,1)}, u32[]{:S(2)}, u32[]{:S(2)}) collective-permute-start(bf16[2,2,96,768]{3,2,1,0:T(8,128)(2,1)} %fusion.184), channel_id=1, source_target_pairs={{0,2},{1,3},{2,0},{3,1},{4,6},{5,7},{6,4},{7,5},{8,10},{9,11},{10,... | collective-permute-start | bytes 1769480 | tf_op jit(solution)/shard_map/ppermute | solution.py:88
  573.5 60.5 %collective-permute-start.77 = (f32[2,96,768]{2,1,0:T(8,128)}, f32[2,96,768]{2,1,0:T(8,128)}, u32[]{:S(2)}, u32[]{:S(2)}) collective-permute-start(f32[2,96,768]{2,1,0:T(8,128)} %slice_bitcast_fusion.11), channel_id=1, source_target_pairs={{0,1},{1,0},{2,3},{3,2},{4,5},{5,4},{6,7},{7,6},{8,9},{9,8},{10,11... | collective-permute-start | bytes 1769480 | tf_op jit(solution)/shard_map/ppermute | solution.py:88
  573.5 39.8 %collective-permute-start.88 = (bf16[96,768]{1,0:T(8,128)(2,1)}, bf16[96,768]{1,0:T(8,128)(2,1)S(1)}, u32[]{:S(2)}, u32[]{:S(2)}) collective-permute-start(bf16[96,768]{1,0:T(8,128)(2,1)} %fusion.236), channel_id=1, source_target_pairs={{0,8},{8,0},{1,9},{9,1},{2,10},{10,2},{3,11},{11,3},{4,12},{12,4},... | collective-permute-start | bytes 442376 | tf_op jit(solution)/shard_map/ppermute | solution.py:88
  632.8 41.0 %collective-permute-start.70 = (f32[32,768]{1,0:T(8,128)}, f32[32,768]{1,0:T(8,128)}, u32[]{:S(2)}, u32[]{:S(2)}) collective-permute-start(f32[32,768]{1,0:T(8,128)} %add.606), channel_id=1, source_target_pairs={{0,2},{1,3},{2,0},{3,1},{4,6},{5,7},{6,4},{7,5},{8,10},{9,11},{10,... | collective-permute-start | bytes 294920 | tf_op jit(solution)/shard_map/ppermute | solution.py:88
  753.7 76.1 %all-to-all-start.3 = ((f32[32,96,192]{2,1,0:T(8,128)}), f32[32,96,192]{2,1,0:T(8,128)S(1)}, u32[]{:S(2)}, u32[]{:S(2)}) async-start(f32[32,96,192]{2,1,0:T(8,128)} %bitcast.869), calls=%async_computation.3 | async-start | bytes 6291456 | tf_op jit(solution)/shard_map/all_to_all | solution.py:811
  948.9 41.2 %all-to-all-start.4 = ((bf16[32,96,192]{2,1,0:T(8,128)(2,1)}), bf16[32,96,192]{2,1,0:T(8,128)(2,1)S(1)}, u32[]{:S(2)}, u32[]{:S(2)}) async-start(bf16[32,96,192]{2,1,0:T(8,128)(2,1)} %bitcast.323), calls=%async_computation.4 | async-start | bytes 3145728 | tf_op jit(solution)/shard_map/all_to_all | solution.py:819
  (294 other events, 3480.3 us)

commit v3 on v2

--- a/solution.py
+++ b/solution.py
@@ -664,6 +664,28 @@
         mod_rows[:, layer_index * 6 * D : (layer_index + 1) * 6 * D].reshape(seq_count, 6, D)
         for layer_index in range(LAYERS)
     ]
+    group = dp_count // 2
+    piece_cols = up_proj.shape[2] // group
+    momenta = oriented(qkv_momentum, out_momentum, up_momentum, down_momentum)
+
+    def cut(matrix):
+        pieces = matrix.reshape(row_count, group, matrix.shape[1] // group)
+        pieces = pieces.transpose(1, 0, 2)
+        return jnp.pad(pieces, ((0, 0), (0, 0), (0, piece_cols - pieces.shape[2])))
+
+    def to_sent(layers):
+        sent = []
+        for layer in layers:
+            up, down, rest = [piece.astype(low) for piece in layer]
+            sent += [cut(up), cut(down), cut(rest[:, :width_qkv]), cut(rest[:, width_qkv:])]
+        return jnp.stack(sent).reshape(dp_count * mp_count, row_count, piece_cols)
+
+    def to_owner(sent):
+        got = lax.all_to_all(sent, MATS, split_axis=0, concat_axis=0, tiled=True)
+        got = got.reshape(2, mp_count, group, row_count, piece_cols).transpose(0, 2, 3, 1, 4)
+        return got.reshape(2 * group * row_count, mp_count * piece_cols)
+
+    sent_momentum = to_sent(momenta)
     saved_all = []
     weights_all = []
     if fast:
@@ -685,6 +707,10 @@
             stream, weights_all[layer_index], layer_mods[layer_index], between
         )
         saved_all.append((saved_a, saved_b))
+        if layer_index == 0:
+            stream, sent_momentum = lax.optimization_barrier((stream, sent_momentum))
+            rows_momentum = to_owner(sent_momentum)
+    stream, rows_momentum = lax.optimization_barrier((stream, rows_momentum))
     base = 6 * LAYERS * D
     shift_f = mod_rows[:, None, base : base + D]
     scale_f = mod_rows[:, None, base + D : base + 2 * D]
@@ -772,7 +798,10 @@
     )
     scalars = jnp.stack([shared_square + own_square, loss_part])
     scalars = jnp.broadcast_to(jnp.pad(scalars, (0, 126))[None], (8, 128))
+    scalars, sent_grads = lax.optimization_barrier((scalars, to_sent(layer_grads)))
+    rows_grad = to_owner(sent_grads)
     scalars = exchange_sum(scalars, order[::-1])
+    scalars, rows_grad = lax.optimization_barrier((scalars, rows_grad))
     square_total, loss = (scalars[0, 0], scalars[0, 1])
     grad_norm = jnp.sqrt(square_total)
     factor = jnp.minimum(1.0, clip_norm / (grad_norm + 1e-06))
@@ -787,30 +816,12 @@
         modulation, grad_mod * factor, mod_first, mod_second, rate_modulation, step_value
     )
 
-    momenta = oriented(qkv_momentum, out_momentum, up_momentum, down_momentum)
     momenta_new = [
         [muon_mu * momentum + factor * grad for momentum, grad in zip(old, new)]
         for old, new in zip(momenta, layer_grads)
     ]
-    pushes = [
-        [factor * grad + muon_mu * momentum for momentum, grad in zip(new_momentum, new)]
-        for new_momentum, new in zip(momenta_new, layer_grads)
-    ]
-    group = dp_count // 2
-    piece_cols = up_proj.shape[2] // group
-
-    def cut(matrix):
-        pieces = matrix.reshape(row_count, group, matrix.shape[1] // group)
-        pieces = pieces.transpose(1, 0, 2)
-        return jnp.pad(pieces, ((0, 0), (0, 0), (0, piece_cols - pieces.shape[2])))
-
-    sent = []
-    for up, down, rest in pushes:
-        sent += [cut(up), cut(down), cut(rest[:, :width_qkv]), cut(rest[:, width_qkv:])]
-    sent = jnp.stack(sent).reshape(dp_count * mp_count, row_count, piece_cols)
-    got = lax.all_to_all(sent, MATS, split_axis=0, concat_axis=0, tiled=True)
-    got = got.reshape(2, mp_count, group, row_count, piece_cols).transpose(0, 2, 3, 1, 4)
-    matrix = got.reshape(2 * group * row_count, mp_count * piece_cols)
+    matrix = (1.0 + muon_mu) * factor * rows_grad.astype(jnp.float32)
+    matrix = matrix + muon_mu * muon_mu * rows_momentum.astype(jnp.float32)
     gram = gram_sum(mat_dot(matrix, matrix.T))
     polar = polar_factor(gram)
     ortho = mat_dot(polar, matrix).astype(low)

time: 1010 us -> 1050 us (1.040)
  waiting for transfers between devices: 378 us -> 334 us
  local copies, waits for them, and re-layouts: 151 us -> 176 us
  other arithmetic: 111 us -> 135 us
  starting transfers between devices: 98.8 us -> 118 us
    all_to_all x1 -> x2, waiting for transfers between devices: 72.4 us -> 25.3 us  [to_owner(): got = lax.all_to_all(sent, MATS, split_axis=0, concat_axis=0, tiled=True)]
    ppermute x98, starting transfers between devices: 82 us -> 95.3 us  [swap(): lax.ppermute(value, axis, [(place, place ^ 1 << bit) for place in range(l...]
    unnamed x458 -> x477, local copies, waits for them, and re-layouts: 45.3 us -> 45.9 us
  transfers between devices with their start and end apart: 103 -> 104, of which waited for: 41 -> 37; matrix products, arithmetic and copies ran while one was open for 26% -> 32% of each run, Pallas kernels for 8% -> 8%
where the time goes in v3:
time: 1050 us; the launch traced here: 1040 us
  waiting for transfers between devices  334 us (32%)
  local copies, waits for them, and re-layouts  176 us (17%)
  matrix products  165 us (16%)
  other arithmetic  135 us (13%)
  starting transfers between devices  118 us (11%)
  Pallas kernels  92.5 us (9%)
  between operations  14.7 us (1%)
    ppermute x98, waiting for transfers between devices, swap(): lax.ppermute(value, axis, [(place, place ^ 1 << bit) for place in range(l...  276 us
    ppermute x98, starting transfers between devices, swap(): lax.ppermute(value, axis, [(place, place ^ 1 << bit) for place in range(l...  95.3 us
    dot_general x16, matrix products, product(): return jnp.einsum(spec, left, right, preferred_element_type=jnp.float32)  66.7 us
    dot_general x19, matrix products, mat_dot(): return jnp.dot(left, right, precision=lax.Precision.HIGH)  65.8 us
    pallas_call x6, Pallas kernels, assemble(): pl.pallas_call(kernel, out_shape=[jax.ShapeDtypeStruct((mp_count, pairs,...  52.1 us
    unnamed x477, local copies, waits for them, and re-layouts  45.9 us
    pallas_call x6, Pallas kernels, weight_grads(): pl.pallas_call(kernel, out_shape=(jax.ShapeDtypeStruct(shape, jnp.float32...  40.4 us
    all_to_all x2, waiting for transfers between devices, to_owner(): got = lax.all_to_all(sent, MATS, split_axis=0, concat_axis=0, tiled=True)  25.3 us
  transfers between devices with their start and end apart: 104, of which 37 were waited for; matrix products, arithmetic and copies ran while one was open for 32% of the time, Pallas kernels for 8%

profile of v3, /device:TPU:0, one launch (start us, length us, event | category | flops | bytes accessed | tf_op | source)
XLA Modules:
  0.0 1035.1 jit_solution(1394666445243421367)
XLA Ops:
  64.6 8.6 collective-permute-done.9
  79.1 11.6 %collective-permute-done.17 = bf16[96,768]{1,0:T(8,128)(2,1)S(1)} collective-permute-done((bf16[96,768]{1,0:T(8,128)(2,1)S(1)}, bf16[96,768]{1,0:T(8,128)(2,1)S(1)}, u32[]{:S(2)}, u32[]{:S(2)}) %collective-permute-start.17) | collective-permute-done | bytes 147488 | tf_op jit(solution)/shard_map/ppermute | solution.py:88
  94.7 8.6 collective-permute-done.13
  104.5 11.4 %collective-permute-done.12 = bf16[2,2,96,768]{3,2,1,0:T(8,128)(2,1)S(1)} collective-permute-done((bf16[2,2,96,768]{3,2,1,0:T(8,128)(2,1)S(1)}, bf16[2,2,96,768]{3,2,1,0:T(8,128)(2,1)S(1)}, u32[]{:S(2)}, u32[]{:S(2)}) %collective-permute-start.12) | collective-permute-done | bytes 589856 | tf_op jit(solution)/shard_map/ppermute | solution.py:88
  126.4 24.8 %collective-permute-done.21 = bf16[2,96,768]{2,1,0:T(8,128)(2,1)} collective-permute-done((bf16[2,96,768]{2,1,0:T(8,128)(2,1)}, bf16[2,96,768]{2,1,0:T(8,128)(2,1)}, u32[]{:S(2)}, u32[]{:S(2)}) %collective-permute-start.21) | collective-permute-done | bytes 294944 | tf_op jit(solution)/shard_map/ppermute | solution.py:88
  171.9 8.9 collective-permute-done.28
  186.8 8.4 collective-permute-done.27
  200.2 9.1 assemble.6
  222.2 8.2 assemble.7
  239.0 8.6 assemble.8
  271.4 24.4 %all-to-all-done.2 = bf16[32,96,192]{2,1,0:T(8,128)(2,1)} async-done(((bf16[32,96,192]{2,1,0:T(8,128)(2,1)}), bf16[32,96,192]{2,1,0:T(8,128)(2,1)}, u32[]{:S(2)}, u32[]{:S(2)}) %all-to-all-start.2) | async-done | bytes 1179680 | tf_op jit(solution)/shard_map/all_to_all | solution.py:684
  311.1 9.1 assemble.9
  330.2 8.1 assemble.10
  346.9 9.0 assemble.11
  449.0 13.6 %collective-permute-done.47 = bf16[2,2,2,96,768]{4,3,2,1,0:T(8,128)(2,1)} collective-permute-done((bf16[2,2,2,96,768]{4,3,2,1,0:T(8,128)(2,1)}, bf16[2,2,2,96,768]{4,3,2,1,0:T(8,128)(2,1)}, u32[]{:S(2)}, u32[]{:S(2)}) %collective-permute-start.47) | collective-permute-done | bytes 1179680 | tf_op jit(solution)/shard_map/ppermute | solution.py:88
  524.4 9.3 collective-permute-done.53
  580.8 20.8 %collective-permute-done.58 = bf16[2,96,768]{2,1,0:T(8,128)(2,1)S(1)} collective-permute-done((bf16[2,96,768]{2,1,0:T(8,128)(2,1)S(1)}, bf16[2,96,768]{2,1,0:T(8,128)(2,1)S(1)}, u32[]{:S(2)}, u32[]{:S(2)}) %collective-permute-start.58) | collective-permute-done | bytes 294944 | tf_op jit(solution)/shard_map/ppermute | solution.py:88
  606.5 24.3 %collective-permute-done.61 = bf16[2,2,2,96,768]{4,3,2,1,0:T(8,128)(2,1)S(1)} collective-permute-done((bf16[2,2,2,96,768]{4,3,2,1,0:T(8,128)(2,1)S(1)}, bf16[2,2,2,96,768]{4,3,2,1,0:T(8,128)(2,1)S(1)}, u32[]{:S(2)}, u32[]{:S(2)}) %collective-permute-start.61) | collective-permute-done | bytes 1179680 | tf_op jit(solution)/shard_map/ppermute | solution.py:88
  666.5 10.4 %all-to-all-done.3 = bf16[32,2,1344]{2,1,0:T(2,128)(2,1)} async-done(((bf16[32,2,1344]{2,1,0:T(2,128)(2,1)}), bf16[32,2,1344]{2,1,0:T(2,128)(2,1)}, u32[]{:S(2)}, u32[]{:S(2)}) %all-to-all-start.3) | async-done | bytes 172064 | tf_op jit(solution)/shard_map/all_to_all | solution.py:777
  741.8 15.9 %collective-permute-done.80 = bf16[2,96,768]{2,1,0:T(8,128)(2,1)S(1)} collective-permute-done((bf16[2,96,768]{2,1,0:T(8,128)(2,1)}, bf16[2,96,768]{2,1,0:T(8,128)(2,1)S(1)}, u32[]{:S(2)}, u32[]{:S(2)}) %collective-permute-start.80) | collective-permute-done | bytes 294944 | tf_op jit(solution)/shard_map/ppermute | solution.py:88
  784.8 8.7 collective-permute-done.86
  824.4 11.4 %collective-permute-done.93 = f32[8,128]{1,0:T(8,128)S(1)} collective-permute-done((f32[8,128]{1,0:T(8,128)S(1)}, f32[8,128]{1,0:T(8,128)S(1)}, u32[]{:S(2)}, u32[]{:S(2)}) %collective-permute-start.93) | collective-permute-done | bytes 4128 | tf_op jit(solution)/shard_map/ppermute | solution.py:88
  868.5 24.7 %collective-permute-done.96 = f32[384,768]{1,0:T(8,128)} collective-permute-done((f32[384,768]{1,0:T(8,128)S(1)}, f32[384,768]{1,0:T(8,128)}, u32[]{:S(2)}, u32[]{:S(2)}) %collective-permute-start.96) | collective-permute-done | bytes 1179680 | tf_op jit(solution)/shard_map/ppermute | solution.py:88
  999.4 23.0 %all-to-all-done.5 = bf16[32,96,192]{2,1,0:T(8,128)(2,1)S(1)} async-done(((bf16[32,96,192]{2,1,0:T(8,128)(2,1)}), bf16[32,96,192]{2,1,0:T(8,128)(2,1)S(1)}, u32[]{:S(2)}, u32[]{:S(2)}) %all-to-all-start.5) | async-done | bytes 1179680 | tf_op jit(solution)/shard_map/all_to_all | solution.py:830
  (1054 shorter events, 699.4 us)
Async XLA Ops:
  5.5 44.6 %collective-permute-start.6 = (bf16[96,768]{1,0:T(8,128)(2,1)S(1)}, bf16[96,768]{1,0:T(8,128)(2,1)}, u32[]{:S(2)}, u32[]{:S(2)}) collective-permute-start(bf16[96,768]{1,0:T(8,128)(2,1)S(1)} %get-tuple-element.106), channel_id=1, source_target_pairs={{0,16},{16,0},{1,17},{17,1},{2,18},{18,2},{3,19},{19,3},{4,20},{20... | collective-permute-start | bytes 442376 | tf_op jit(solution)/shard_map/ppermute | solution.py:88
  8.6 42.5 %collective-permute-start.7 = (bf16[96,768]{1,0:T(8,128)(2,1)S(1)}, bf16[96,768]{1,0:T(8,128)(2,1)}, u32[]{:S(2)}, u32[]{:S(2)}) collective-permute-start(bf16[96,768]{1,0:T(8,128)(2,1)S(1)} %get-tuple-element.107), channel_id=1, source_target_pairs={{0,8},{8,0},{1,9},{9,1},{2,10},{10,2},{3,11},{11,3},{4,12},{12,4},... | collective-permute-start | bytes 442376 | tf_op jit(solution)/shard_map/ppermute | solution.py:88
  10.1 42.0 %collective-permute-start.8 = (bf16[96,768]{1,0:T(8,128)(2,1)S(1)}, bf16[96,768]{1,0:T(8,128)(2,1)}, u32[]{:S(2)}, u32[]{:S(2)}) collective-permute-start(bf16[96,768]{1,0:T(8,128)(2,1)S(1)} %pad_maximum_fusion.27), channel_id=1, source_target_pairs={{0,2},{1,3},{2,0},{3,1},{4,6},{5,7},{6,4},{7,5},{8,10},{9,11},{10,... | collective-permute-start | bytes 442376 | tf_op jit(solution)/shard_map/ppermute | solution.py:88
  42.7 80.8 %all-to-all-start = ((f32[8,32,96]{2,1,0:T(8,128)}), f32[8,32,96]{2,1,0:T(8,128)}, u32[]{:S(2)}, u32[]{:S(2)}) async-start(f32[8,32,96]{2,1,0:T(8,128)} %bitcast.902), calls=%async_computation | async-start | bytes 262144 | tf_op jit(solution)/shard_map/all_to_all | solution.py:637
  117.0 43.1 %collective-permute-start.18 = (bf16[2,2,2,96,768]{4,3,2,1,0:T(8,128)(2,1)S(1)}, bf16[2,2,2,96,768]{4,3,2,1,0:T(8,128)(2,1)}, u32[]{:S(2)}, u32[]{:S(2)}) collective-permute-start(bf16[2,2,2,96,768]{4,3,2,1,0:T(8,128)(2,1)S(1)} %pad_maximum_fusion.5.refs_0_), channel_id=1, source_target_pairs={{0,16},{16,0},{1,17},{17,1},{2,18},{18,2},{3,19},{19,3},{4,20},{20... | collective-permute-start | bytes 3538952 | tf_op jit(solution)/shard_map/ppermute | solution.py:88
  119.2 44.8 %collective-permute-start.25 = (bf16[2,2,2,96,768]{4,3,2,1,0:T(8,128)(2,1)}, bf16[2,2,2,96,768]{4,3,2,1,0:T(8,128)(2,1)}, u32[]{:S(2)}, u32[]{:S(2)}) collective-permute-start(bf16[2,2,2,96,768]{4,3,2,1,0:T(8,128)(2,1)} %pad_maximum_fusion.4.refs_0_), channel_id=1, source_target_pairs={{0,1},{1,0},{2,3},{3,2},{4,5},{5,4},{6,7},{7,6},{8,9},{9,8},{10,11... | collective-permute-start | bytes 3538952 | tf_op jit(solution)/shard_map/ppermute | solution.py:88
  119.2 44.8 %collective-permute-start.24 = (bf16[2,2,2,96,768]{4,3,2,1,0:T(8,128)(2,1)}, bf16[2,2,2,96,768]{4,3,2,1,0:T(8,128)(2,1)}, u32[]{:S(2)}, u32[]{:S(2)}) collective-permute-start(bf16[2,2,2,96,768]{4,3,2,1,0:T(8,128)(2,1)} %pad_maximum_fusion.3.refs_0_), channel_id=1, source_target_pairs={{0,8},{8,0},{1,9},{9,1},{2,10},{10,2},{3,11},{11,3},{4,12},{12,4},... | collective-permute-start | bytes 3538952 | tf_op jit(solution)/shard_map/ppermute | solution.py:88
  180.8 58.2 %collective-permute-start.31 = (bf16[2,2,2,96,768]{4,3,2,1,0:T(8,128)(2,1)}, bf16[2,2,2,96,768]{4,3,2,1,0:T(8,128)(2,1)}, u32[]{:S(2)}, u32[]{:S(2)}) collective-permute-start(bf16[2,2,2,96,768]{4,3,2,1,0:T(8,128)(2,1)} %pad_maximum_fusion.4.refs_0_), channel_id=1, source_target_pairs={{0,4},{4,0},{1,5},{5,1},{2,6},{6,2},{3,7},{7,3},{8,12},{12,8},{9,1... | collective-permute-start | bytes 3538952 | tf_op jit(solution)/shard_map/ppermute | solution.py:88
  197.5 41.5 %collective-permute-start.32 = (bf16[2,2,2,96,768]{4,3,2,1,0:T(8,128)(2,1)}, bf16[2,2,2,96,768]{4,3,2,1,0:T(8,128)(2,1)}, u32[]{:S(2)}, u32[]{:S(2)}) collective-permute-start(bf16[2,2,2,96,768]{4,3,2,1,0:T(8,128)(2,1)} %collective-permute-done.25.refs_1_), channel_id=1, source_target_pairs={{0,4},{4,0},{1,5},{5,1},{2,6},{6,2},{3,7},{7,3},{8,12},{12,8},{9,1... | collective-permute-start | bytes 3538952 | tf_op jit(solution)/shard_map/ppermute | solution.py:88
  253.2 42.6 %all-to-all-start.2 = ((bf16[32,96,192]{2,1,0:T(8,128)(2,1)}), bf16[32,96,192]{2,1,0:T(8,128)(2,1)}, u32[]{:S(2)}, u32[]{:S(2)}) async-start(bf16[32,96,192]{2,1,0:T(8,128)(2,1)} %bitcast.903), calls=%async_computation.2 | async-start | bytes 3145728 | tf_op jit(solution)/shard_map/all_to_all | solution.py:684
  257.1 46.5 %collective-permute-start.34 = (bf16[2,2,2,96,768]{4,3,2,1,0:T(8,128)(2,1)}, bf16[2,2,2,96,768]{4,3,2,1,0:T(8,128)(2,1)}, u32[]{:S(2)}, u32[]{:S(2)}) collective-permute-start(bf16[2,2,2,96,768]{4,3,2,1,0:T(8,128)(2,1)} %pad_maximum_fusion.8.refs_0_), channel_id=1, source_target_pairs={{0,4},{4,0},{1,5},{5,1},{2,6},{6,2},{3,7},{7,3},{8,12},{12,8},{9,1... | collective-permute-start | bytes 3538952 | tf_op jit(solution)/shard_map/ppermute | solution.py:88
  257.6 53.0 %collective-permute-start.39 = (bf16[2,2,2,96,768]{4,3,2,1,0:T(8,128)(2,1)}, bf16[2,2,2,96,768]{4,3,2,1,0:T(8,128)(2,1)}, u32[]{:S(2)}, u32[]{:S(2)}) collective-permute-start(bf16[2,2,2,96,768]{4,3,2,1,0:T(8,128)(2,1)} %pad_maximum_fusion.7.refs_0_), channel_id=1, source_target_pairs={{0,1},{1,0},{2,3},{3,2},{4,5},{5,4},{6,7},{7,6},{8,9},{9,8},{10,11... | collective-permute-start | bytes 3538952 | tf_op jit(solution)/shard_map/ppermute | solution.py:88
  259.2 51.4 %collective-permute-start.36 = (bf16[2,2,2,96,768]{4,3,2,1,0:T(8,128)(2,1)}, bf16[2,2,2,96,768]{4,3,2,1,0:T(8,128)(2,1)}, u32[]{:S(2)}, u32[]{:S(2)}) collective-permute-start(bf16[2,2,2,96,768]{4,3,2,1,0:T(8,128)(2,1)} %pad_maximum_fusion.6.refs_0_), channel_id=1, source_target_pairs={{0,8},{8,0},{1,9},{9,1},{2,10},{10,2},{3,11},{11,3},{4,12},{12,4},... | collective-permute-start | bytes 3538952 | tf_op jit(solution)/shard_map/ppermute | solution.py:88
  260.7 50.4 %collective-permute-start.35 = (bf16[2,2,2,96,768]{4,3,2,1,0:T(8,128)(2,1)}, bf16[2,2,2,96,768]{4,3,2,1,0:T(8,128)(2,1)}, u32[]{:S(2)}, u32[]{:S(2)}) collective-permute-start(bf16[2,2,2,96,768]{4,3,2,1,0:T(8,128)(2,1)} %collective-permute-done.33.refs_1_), channel_id=1, source_target_pairs={{0,4},{4,0},{1,5},{5,1},{2,6},{6,2},{3,7},{7,3},{8,12},{12,8},{9,1... | collective-permute-start | bytes 3538952 | tf_op jit(solution)/shard_map/ppermute | solution.py:88
  266.5 80.4 %collective-permute-start.40 = (bf16[2,2,2,96,768]{4,3,2,1,0:T(8,128)(2,1)}, bf16[2,2,2,96,768]{4,3,2,1,0:T(8,128)(2,1)}, u32[]{:S(2)}, u32[]{:S(2)}) collective-permute-start(bf16[2,2,2,96,768]{4,3,2,1,0:T(8,128)(2,1)} %pad_maximum_fusion.7.refs_0_), channel_id=1, source_target_pairs={{0,4},{4,0},{1,5},{5,1},{2,6},{6,2},{3,7},{7,3},{8,12},{12,8},{9,1... | collective-permute-start | bytes 3538952 | tf_op jit(solution)/shard_map/ppermute | solution.py:88
  310.5 194.5 %collective-permute-start.57 = (bf16[4,256,768]{2,1,0:T(8,128)(2,1)}, bf16[4,256,768]{2,1,0:T(8,128)(2,1)}, u32[]{:S(2)}, u32[]{:S(2)}) collective-permute-start(bf16[4,256,768]{2,1,0:T(8,128)(2,1)} %get-tuple-element.453.refs_2_), channel_id=1, source_target_pairs={{0,4},{4,0},{1,5},{5,1},{2,6},{6,2},{3,7},{7,3},{8,12},{12,8},{9,1... | collective-permute-start | bytes 4718600 | tf_op jit(solution)/shard_map/ppermute | solution.py:88
  346.3 52.2 %collective-permute-start.45 = (bf16[4,256,768]{2,1,0:T(8,128)(2,1)}, bf16[4,256,768]{2,1,0:T(8,128)(2,1)}, u32[]{:S(2)}, u32[]{:S(2)}) collective-permute-start(bf16[4,256,768]{2,1,0:T(8,128)(2,1)} %get-tuple-element.460.refs_2_), channel_id=1, source_target_pairs={{0,4},{4,0},{1,5},{5,1},{2,6},{6,2},{3,7},{7,3},{8,12},{12,8},{9,1... | collective-permute-start | bytes 4718600 | tf_op jit(solution)/shard_map/ppermute | solution.py:88
  560.7 72.7 %collective-permute-start.65 = (bf16[4,256,768]{2,1,0:T(8,128)(2,1)}, bf16[4,256,768]{2,1,0:T(8,128)(2,1)}, u32[]{:S(2)}, u32[]{:S(2)}) collective-permute-start(bf16[4,256,768]{2,1,0:T(8,128)(2,1)} %pad_maximum_fusion.2.refs_4_), channel_id=1, source_target_pairs={{0,4},{4,0},{1,5},{5,1},{2,6},{6,2},{3,7},{7,3},{8,12},{12,8},{9,1... | collective-permute-start | bytes 4718600 | tf_op jit(solution)/shard_map/ppermute | solution.py:88
  561.7 71.7 %collective-permute-start.64 = (bf16[4,96,256]{2,1,0:T(8,128)(2,1)}, bf16[4,96,256]{2,1,0:T(8,128)(2,1)}, u32[]{:S(2)}, u32[]{:S(2)}) collective-permute-start(bf16[4,96,256]{2,1,0:T(8,128)(2,1)} %get-tuple-element.389), channel_id=1, source_target_pairs={{0,4},{4,0},{1,5},{5,1},{2,6},{6,2},{3,7},{7,3},{8,12},{12,8},{9,1... | collective-permute-start | bytes 589832 | tf_op jit(solution)/shard_map/ppermute | solution.py:88
  641.3 87.7 %collective-permute-start.79 = (bf16[2,2,2,96,768]{4,3,2,1,0:T(8,128)(2,1)}, bf16[2,2,2,96,768]{4,3,2,1,0:T(8,128)(2,1)}, u32[]{:S(2)}, u32[]{:S(2)}) collective-permute-start(bf16[2,2,2,96,768]{4,3,2,1,0:T(8,128)(2,1)} %get-tuple-element.178), channel_id=1, source_target_pairs={{0,16},{16,0},{1,17},{17,1},{2,18},{18,2},{3,19},{19,3},{4,20},{20... | collective-permute-start | bytes 3538952 | tf_op jit(solution)/shard_map/ppermute | solution.py:88
  642.8 76.2 %collective-permute-start.78 = (bf16[2,2,96,768]{3,2,1,0:T(8,128)(2,1)}, bf16[2,2,96,768]{3,2,1,0:T(8,128)(2,1)}, u32[]{:S(2)}, u32[]{:S(2)}) collective-permute-start(bf16[2,2,96,768]{3,2,1,0:T(8,128)(2,1)} %fusion.189), channel_id=1, source_target_pairs={{0,2},{1,3},{2,0},{3,1},{4,6},{5,7},{6,4},{7,5},{8,10},{9,11},{10,... | collective-permute-start | bytes 1769480 | tf_op jit(solution)/shard_map/ppermute | solution.py:88
  646.1 70.0 %collective-permute-start.77 = (f32[2,96,768]{2,1,0:T(8,128)}, f32[2,96,768]{2,1,0:T(8,128)}, u32[]{:S(2)}, u32[]{:S(2)}) collective-permute-start(f32[2,96,768]{2,1,0:T(8,128)} %slice_bitcast_fusion.11), channel_id=1, source_target_pairs={{0,1},{1,0},{2,3},{3,2},{4,5},{5,4},{6,7},{7,6},{8,9},{9,8},{10,11... | collective-permute-start | bytes 1769480 | tf_op jit(solution)/shard_map/ppermute | solution.py:88
  805.7 42.2 %all-to-all-start.4 = ((bf16[32,96,192]{2,1,0:T(8,128)(2,1)}), bf16[32,96,192]{2,1,0:T(8,128)(2,1)S(1)}, u32[]{:S(2)}, u32[]{:S(2)}) async-start(bf16[32,96,192]{2,1,0:T(8,128)(2,1)} %bitcast.342), calls=%async_computation.4 | async-start | bytes 3145728 | tf_op jit(solution)/shard_map/all_to_all | solution.py:684
  981.1 41.2 %all-to-all-start.5 = ((bf16[32,96,192]{2,1,0:T(8,128)(2,1)}), bf16[32,96,192]{2,1,0:T(8,128)(2,1)S(1)}, u32[]{:S(2)}, u32[]{:S(2)}) async-start(bf16[32,96,192]{2,1,0:T(8,128)(2,1)} %bitcast.348), calls=%async_computation.5 | async-start | bytes 3145728 | tf_op jit(solution)/shard_map/all_to_all | solution.py:830
  (301 other events, 3730.8 us)
